TPU v7x, 512 devices: a whole 4x4x16 slice. The times are simulated.
512 devices in a mesh: az: 32 (over z, x_lo), rad: 16 (over y, x_hi, core).
Axes of the slice: x: 4 (x_hi: 2, x_lo: 2; x = x_hi * 2 + x_lo), y: 4, z: 16, core: 2. Of those that a mesh axis runs over, the one named last changes fastest.
Arguments:
- potential: float32 [3, 3, 8192, 2048], P(None, None, 'az', 'rad'), may hold values from -6 to 6
- current: float32 [3, 3, 8192, 2048], P(None, None, 'az', 'rad'), may hold values from -24 to 24
- material: int32 [3, 8192, 2048], P(None, 'az', 'rad'), may hold values from 0 to 7
- nu_table: float32 [8], replicated, may hold values from 0.2 to 2
- sat_table: float32 [8], replicated, may hold values from 0.2 to 3
- panel_flux: float32 [9, 8192], P(None, 'az'), may hold values from -48 to 48
- panel_jitter: int32 [8192], P('az'), may hold values from 0 to 8191
- rotor_offset: int32 [1], replicated, may hold values from 0 to 8191
Outputs:
- updated: float32 [3, 3, 8192, 2048], P(None, None, 'az', 'rad')
All inputs are finite; a program needn't handle non-finite values.
Results may differ from a plain program's by a relative error of at most 0.000064.
Values sent between devices are 32-bit elements; how exact they have to be, the bound alone decides.
A program may use at most 64 MiB of HBM per device.

v0:
```python
import jax
import jax.numpy as jnp
from jax import lax
from jax.sharding import PartitionSpec as P

sigma_term = 1.0
neighbour_steps = ((0, 1, 0), (0, -1, 0), (0, 0, 1), (0, 0, -1), (1, 0, 0), (-1, 0, 0))


def with_halo(x, sides, width, wrap):
    for axis, dim in sides:
        peers, length = (lax.axis_size(axis), x.shape[dim])
        up = [(i, (i + 1) % peers) for i in range(peers if wrap else peers - 1)]
        down = [(j, i) for i, j in up]
        last = lax.slice_in_dim(x, length - width, length, axis=dim)
        first = lax.slice_in_dim(x, 0, width, axis=dim)
        before = lax.ppermute(last, axis, up)
        after = lax.ppermute(first, axis, down)
        x = jnp.concatenate([before, x, after], axis=dim)
    return x


def lookup(material, values_table):
    result = jnp.zeros(material.shape, values_table.dtype)
    for entry in range(values_table.shape[0]):
        result = result + jnp.where(
            material == entry, values_table[entry], jnp.zeros((), values_table.dtype)
        )
    return result


def extend_cells(field, width):
    widened = with_halo(field, (("az", 2),), width, True)
    return with_halo(widened, (("rad", 3),), width, False)


def strength(extended):
    centre = extended[:, :, 1:-1, 1:-1]
    azimuth_diff = extended[:, :, 2:, 1:-1] - centre
    radial_diff = extended[:, :, 1:-1, 2:] - centre
    return jnp.sum(azimuth_diff * azimuth_diff + radial_diff * radial_diff, axis=0, keepdims=True)


def offset_view(field, layer_step, az_step, rad_step):
    return field[
        :,
        1 + layer_step : field.shape[1] - 1 + layer_step,
        1 + az_step : field.shape[2] - 1 + az_step,
        1 + rad_step : field.shape[3] - 1 + rad_step,
    ]


def jacobi_sweep(field, coef, source):
    padded_field = jnp.pad(field, ((0, 0), (1, 1), (0, 0), (0, 0)))
    padded_coef = jnp.pad(coef, ((0, 0), (1, 1), (0, 0), (0, 0)))
    centre = offset_view(padded_coef, 0, 0, 0)
    numerator = source
    denominator = jnp.full_like(centre, sigma_term)
    for layer_step, az_step, rad_step in neighbour_steps:
        face_coef = 0.5 * (centre + offset_view(padded_coef, layer_step, az_step, rad_step))
        numerator = numerator + face_coef * offset_view(padded_field, layer_step, az_step, rad_step)
        denominator = denominator + face_coef
    return numerator / denominator


def deposit(block_piece, offset, cell_count, cycle_cells, base_cell):
    values = block_piece[:-1]
    jitter = block_piece[-1].astype(jnp.int32)
    position = (offset + jitter) % cycle_cells
    local_cell = position - base_cell
    onehot = (local_cell[:, None] == jnp.arange(cell_count, dtype=jnp.int32)[None, :]).astype(
        jnp.float32
    )
    return jnp.dot(
        values, onehot, precision=lax.Precision.HIGHEST, preferred_element_type=jnp.float32
    )


def local(
    potential, current, material, nu_table, sat_table, panel_flux, panel_jitter, rotor_offset
):
    layers = potential.shape[1]
    tile_cells = potential.shape[2]
    az_count = lax.axis_size("az")
    cycle_cells = tile_cells * az_count
    own_tile = lax.axis_index("az")
    base_cell = own_tile * tile_cells
    offset = rotor_offset[0]
    packed = jnp.concatenate([panel_flux, panel_jitter.astype(jnp.float32)[None, :]], axis=0)
    airgap = deposit(
        lax.all_gather(packed, "az", axis=1, tiled=True), offset, tile_cells, cycle_cells, base_cell
    )
    stator_row = lax.axis_index("rad") == lax.axis_size("rad") // 2
    airgap = jnp.where(stator_row, airgap, 0.0).reshape(3, layers, tile_cells)
    source = current.at[:, :, :, 0].add(airgap)
    base_reluct = lookup(material, nu_table)[None]
    saturation = lookup(material, sat_table)[None]
    extended = extend_cells(potential, 1)
    flux_sq = strength(extended)
    reluct = base_reluct * (1.0 + saturation * flux_sq / (1.0 + flux_sq))
    reluct_wide = extend_cells(reluct, 1)
    sweep_one = jacobi_sweep(extended, reluct_wide, source)
    result = jacobi_sweep(extend_cells(sweep_one, 1), reluct_wide, source)
    return result


def solution(mesh):
    placed = (
        P(None, None, "az", "rad"),
        P(None, None, "az", "rad"),
        P(None, "az", "rad"),
        P(),
        P(),
        P(None, "az"),
        P("az"),
        P(),
    )
    return jax.shard_map(
        local, mesh=mesh, in_specs=placed, out_specs=P(None, None, "az", "rad"), check_vma=False
    )
```

profile of v0, /device:TPU:1, one launch (start us, length us, event | category | flops | bytes accessed | tf_op | source)
XLA Modules:
  0.0 203.8 jit_solution(14559868421932687372)
XLA Ops:
  0.0 2.5 %copy.169 = f32[3,3,256,128]{3,2,1,0:T(8,128)} copy(f32[3,3,256,128]{3,2,1,0:T(8,128)} %param.11) | data formatting | bytes 2359296
  2.5 12.9 %collective-permute-start = (f32[3,3,1,128]{3,1,2,0:T(4,128)S(1)}, f32[3,3,1,128]{3,1,2,0:T(4,128)S(1)}, u32[]{:S(2)}, u32[]{:S(2)}) collective-permute-start(f32[3,3,1,128]{3,1,2,0:T(4,128)S(1)} %copy.164), channel_id=1, source_target_pairs={{16,0},{32,16},{48,32},{64,48},{80,64},{96,80},{112,96},{128,112},... | collective-permute-start | bytes 13832 | tf_op jit(solution)/shard_map/ppermute | solution.py:18
  15.4 1.9 collective-permute-start.1
  18.0 50.8 %all_gather.3 = f32[10,8192]{1,0:T(8,128)S(1)} all-gather(f32[10,256]{1,0:T(8,128)S(1)} %pad_maximum_fusion.26), channel_id=1, replica_groups=mesh['az'=32,'rad'=16] {'az'}, dimensions={1}, use_global_device_ids=true | all-gather | bytes 337920 | tf_op jit(solution)/shard_map/all_gather | solution.py:91
  68.9 0.0 copy-start.15
  68.9 2.7 %fusion.29 = f32[9,256]{1,0:T(8,128)S(1)} fusion(s32[8192]{0:T(1024)S(1)} %fusion.46, f32[10,8192]{1,0:T(8,128)S(1)} %all_gather.3, pred[]{:T(512)S(6)} %eq.50), kind=kOutput, calls=%fused_computation.69 | convolution fusion | flops 228591872 | bytes 369665 | tf_op jit(solution)/shard_map/dot_general | solution.py:74
  71.6 0.7 fusion.55
  72.3 0.0 collective-permute-done
  72.3 0.0 collective-permute-done.1
  72.3 0.1 pad_maximum_fusion
  72.4 1.4 fusion.51
  73.9 2.0 copy.136
  75.9 17.3 %collective-permute-start.2 = (f32[3,3,258,1]{2,1,3,0:T(4,128)S(1)}, f32[3,3,258,1]{2,1,3,0:T(4,128)S(1)}, u32[]{:S(2)}, u32[]{:S(2)}) collective-permute-start(f32[3,3,258,1]{2,1,3,0:T(4,128)S(1)} %copy.136), channel_id=1, source_target_pairs={{1,0},{2,1},{3,2},{4,3},{5,4},{6,5},{7,6},{8,7},{9,8},{10,9},{11,1... | collective-permute-start | bytes 27872 | tf_op jit(solution)/shard_map/ppermute | solution.py:18
  93.2 0.7 fusion.56
  93.9 0.2 copy.123
  94.2 2.1 %reshape.66 = f32[3,3,256,1]{3,2,1,0:T(8,128)} reshape(f32[9,256]{1,0:T(8,128)S(1)} %fusion.29) | data formatting | bytes 18432 | tf_op jit(solution)/shard_map/reshape.29
  96.2 0.7 copy.144
  96.9 4.3 %collective-permute-start.7 = (f32[3,3,258,1]{2,1,3,0:T(4,128)S(1)}, f32[3,3,258,1]{2,1,3,0:T(4,128)S(1)}, u32[]{:S(2)}, u32[]{:S(2)}) collective-permute-start(f32[3,3,258,1]{2,1,3,0:T(4,128)S(1)} %copy.144), channel_id=1, source_target_pairs={{0,1},{1,2},{2,3},{3,4},{4,5},{5,6},{6,7},{7,8},{8,9},{9,10},{10,1... | collective-permute-start | bytes 27872 | tf_op jit(solution)/shard_map/ppermute | solution.py:17
  101.2 0.0 collective-permute-done.2
  101.2 0.4 copy.137
  101.6 0.7 fusion.28
  102.3 1.0 copy.163
  103.3 12.6 %multiply_bitcast_fusion = f32[1,3,256,128]{2,1,3,0:T(4,128)S(1)} fusion(f32[3,256,128]{1,0,2:T(4,128)} %copy.163, s32[3,256,128]{1,0,2:T(4,128)S(1)} %copy.123, f32[]{:T(128)} %bitcast.18, f32[]{:T(128)} %bitcast.17, f32[]{:T(128)} %bitcast.16, f32[]{:T(128)} %bitcast.15, f32[]{:T(128)} %bitcast.14, f32[]{:T(128)} %bitcast.13, f32[]{:T(128)} %bitcast.12, ...), kind=kLoop, calls=%fused_computation.92 | loop fusion | flops 4227072 | bytes 1179712 | tf_op jit(solution)/shard_map/mul | solution.py:100
  115.9 1.0 fusion.54
  116.8 1.9 collective-permute-start.4
  118.8 5.5 %collective-permute-start.3 = (f32[1,3,1,128]{2,1,3,0:T(4,128)}, f32[1,3,1,128]{2,1,3,0:T(4,128)S(1)}, u32[]{:S(2)}, u32[]{:S(2)}) collective-permute-start(f32[1,3,1,128]{2,1,3,0:T(4,128)} %get-tuple-element.35), channel_id=1, source_target_pairs={{16,0},{32,16},{48,32},{64,48},{80,64},{96,80},{112,96},{128,112},... | collective-permute-start | bytes 4616 | tf_op jit(solution)/shard_map/ppermute | solution.py:18
  124.3 1.2 slice_add_fusion
  125.4 4.7 %scatter-add.4 = f32[3,3,256,128]{3,2,1,0:T(8,128)} dynamic-update-slice(f32[3,3,256,128]{3,2,1,0:T(8,128)} %copy.169, f32[3,3,256,1]{3,2,1,0:T(8,128)} %slice_add_fusion, s32[]{:T(128)} %constant.61.clone.1, s32[]{:T(128)} %constant.61.clone.1, s32[]{:T(128)} %constant.61.clone.1, s32[]{:T(128)} %constant.61.clone.1) | dynamic-update-slice | bytes 18436 | tf_op jit(solution)/shard_map/scatter-add | solution.py:95
  130.1 0.0 collective-permute-done.7
  130.1 1.5 copy.145
  131.6 0.0 collective-permute-done.4
  131.6 1.5 collective-permute-done.3
  133.1 0.1 pad_maximum_fusion.27
  133.2 4.6 %collective-permute-start.6 = (f32[1,3,258,1]{2,1,3,0:T(4,128)S(1)}, f32[1,3,258,1]{2,1,3,0:T(4,128)S(1)}, u32[]{:S(2)}, u32[]{:S(2)}) collective-permute-start(f32[1,3,258,1]{2,1,3,0:T(4,128)S(1)} %get-tuple-element.30), channel_id=1, source_target_pairs={{0,1},{1,2},{2,3},{3,4},{4,5},{5,6},{6,7},{7,8},{8,9},{9,10},{10,1... | collective-permute-start | bytes 9296 | tf_op jit(solution)/shard_map/ppermute | solution.py:17
  137.9 2.1 %collective-permute-start.5 = (f32[1,3,258,1]{2,1,3,0:T(4,128)S(1)}, f32[1,3,258,1]{2,1,3,0:T(4,128)S(1)}, u32[]{:S(2)}, u32[]{:S(2)}) collective-permute-start(f32[1,3,258,1]{2,1,3,0:T(4,128)S(1)} %get-tuple-element.31), channel_id=1, source_target_pairs={{1,0},{2,1},{3,2},{4,3},{5,4},{6,5},{7,6},{8,7},{9,8},{10,9},{11,1... | collective-permute-start | bytes 9296 | tf_op jit(solution)/shard_map/ppermute | solution.py:18
  140.0 4.4 %select_maximum_fusion.4 = f32[3,5,258,130]{3,2,1,0:T(8,128)} fusion(f32[3,3,258,1]{3,2,1,0:T(8,128)S(1)} %copy.137, f32[3,3,258,1]{3,2,1,0:T(8,128)} %copy.145, f32[3,3,1,128]{3,2,1,0:T(1,128)S(1)} %copy.132, f32[3,3,256,128]{3,2,1,0:T(8,128)S(1)} %copy-done, f32[3,3,1,128]{3,2,1,0:T(1,128)S(1)} %copy.134), kind=kLoop, calls=%fused_computation.9 | loop fusion | flops 6037200 | bytes 3219840 | tf_op jit(solution)/shard_map/concatenate | solution.py:19
  144.4 0.0 collective-permute-done.6
  144.4 0.0 collective-permute-done.5
  144.4 1.8 fusion.48
  146.1 2.0 copy.142
  148.1 2.0 copy.143
  150.1 2.0 copy.140
  152.1 0.8 select_maximum_fusion.8
  152.9 3.3 %fusion.43 = (f32[3,256,128]{1,0,2:T(4,128)}, f32[3,256,128]{1,0,2:T(4,128)}, f32[3,256,128]{1,0,2:T(4,128)}, f32[3,256,128]{1,0,2:T(4,128)}) fusion(f32[1,3,256,128]{2,1,3,0:T(4,128)S(1)} %multiply_bitcast_fusion, f32[1,5,258,130]{2,1,3,0:T(8,128)S(1)} %select_maximum_fusion.8, f32[1,3,1,128]{2,1,3,0:T(4,128)S(1)} %collective-permute-done.3, ...), kind=kLoop, calls=%fused_computation.96 | loop fusion | flops 2555904 | bytes 2761776 | tf_op jit(solution)/shard_map/mul | solution.py:61
  156.2 2.0 copy.146
  158.2 2.0 copy.150
  160.3 2.0 copy.149
  162.2 2.0 copy.139
  164.2 4.9 %fusion.16 = f32[3,3,256,128]{3,2,1,0:T(8,128)S(1)} fusion(f32[3,5,258,130]{3,2,1,0:T(8,128)} %select_maximum_fusion.4, f32[3,3,258,1]{3,2,1,0:T(8,128)} %copy.145, f32[3,3,1,128]{3,2,1,0:T(1,128)S(1)} %copy.132, f32[3,3,256,128]{3,2,1,0:T(8,128)S(1)} %copy-done, f32[3,3,1,128]{3,2,1,0:T(1,128)S(1)} %copy.134, f32[3,3,256,128]{3,2,1,0:T(8,128)} %scatter-add.4, ...), kind=kLoop, calls=%fused_computation.46 | loop fusion | flops 6193152 | bytes 8678544 | tf_op jit(solution)/shard_map/div | solution.py:63
  169.1 1.9 collective-permute-start.8
  171.1 3.4 %collective-permute-start.9 = (f32[3,3,1,128]{3,1,2,0:T(4,128)S(1)}, f32[3,3,1,128]{3,1,2,0:T(4,128)S(1)}, u32[]{:S(2)}, u32[]{:S(2)}) collective-permute-start(f32[3,3,1,128]{3,1,2,0:T(4,128)S(1)} %copy.153), channel_id=1, source_target_pairs={{0,16},{16,32},{32,48},{48,64},{64,80},{80,96},{96,112},{112,128},... | collective-permute-start | bytes 13832 | tf_op jit(solution)/shard_map/ppermute | solution.py:17
  174.5 3.1 %collective-permute-done.9 = f32[3,3,1,128]{3,1,2,0:T(4,128)S(1)} collective-permute-done((f32[3,3,1,128]{3,1,2,0:T(4,128)S(1)}, f32[3,3,1,128]{3,1,2,0:T(4,128)S(1)}, u32[]{:S(2)}, u32[]{:S(2)}) %collective-permute-start.9) | collective-permute-done | bytes 4640 | tf_op jit(solution)/shard_map/ppermute | solution.py:17
  177.6 0.1 pad_maximum_fusion.1
  177.7 1.4 fusion.50
  179.1 2.0 copy.159
  181.1 7.0 %collective-permute-start.11 = (f32[3,3,258,1]{2,1,3,0:T(4,128)S(1)}, f32[3,3,258,1]{2,1,3,0:T(4,128)S(1)}, u32[]{:S(2)}, u32[]{:S(2)}) collective-permute-start(f32[3,3,258,1]{2,1,3,0:T(4,128)S(1)} %copy.159), channel_id=1, source_target_pairs={{0,1},{1,2},{2,3},{3,4},{4,5},{5,6},{6,7},{7,8},{8,9},{9,10},{10,1... | collective-permute-start | bytes 27872 | tf_op jit(solution)/shard_map/ppermute | solution.py:17
  188.1 0.7 copy.157
  188.8 2.1 %collective-permute-start.10 = (f32[3,3,258,1]{2,1,3,0:T(4,128)S(1)}, f32[3,3,258,1]{2,1,3,0:T(4,128)S(1)}, u32[]{:S(2)}, u32[]{:S(2)}) collective-permute-start(f32[3,3,258,1]{2,1,3,0:T(4,128)S(1)} %copy.157), channel_id=1, source_target_pairs={{1,0},{2,1},{3,2},{4,3},{5,4},{6,5},{7,6},{8,7},{9,8},{10,9},{11,1... | collective-permute-start | bytes 27872 | tf_op jit(solution)/shard_map/ppermute | solution.py:18
  190.8 0.0 collective-permute-done.11
  190.9 0.4 copy.160
  191.3 4.2 %collective-permute-done.10 = f32[3,3,258,1]{2,1,3,0:T(4,128)S(1)} collective-permute-done((f32[3,3,258,1]{2,1,3,0:T(4,128)S(1)}, f32[3,3,258,1]{2,1,3,0:T(4,128)S(1)}, u32[]{:S(2)}, u32[]{:S(2)}) %collective-permute-start.10) | collective-permute-done | bytes 9320 | tf_op jit(solution)/shard_map/ppermute | solution.py:18
  195.5 1.5 copy.158
  197.0 3.3 %select_maximum_fusion = f32[3,5,258,130]{3,2,1,0:T(8,128)S(1)} fusion(f32[3,3,258,1]{3,2,1,0:T(8,128)} %copy.158, f32[3,3,258,1]{3,2,1,0:T(8,128)S(1)} %copy.160, f32[3,3,1,128]{3,2,1,0:T(1,128)S(1)} %copy.152, f32[3,3,256,128]{3,2,1,0:T(8,128)S(1)} %copy-done.2, f32[3,3,1,128]{3,2,1,0:T(1,128)S(1)} %copy.154), kind=kLoop, calls=%fused_computation.5 | loop fusion | flops 6037200 | bytes 3219840 | tf_op jit(solution)/shard_map/concatenate | solution.py:19
  200.4 3.4 %fusion.5 = f32[3,3,256,128]{3,2,1,0:T(8,128)} fusion(f32[3,5,258,130]{3,2,1,0:T(8,128)S(1)} %select_maximum_fusion, f32[3,3,258,1]{3,2,1,0:T(8,128)S(1)} %copy.160, f32[3,3,1,128]{3,2,1,0:T(1,128)S(1)} %copy.152, f32[3,3,256,128]{3,2,1,0:T(8,128)S(1)} %copy-done.2, f32[3,3,1,128]{3,2,1,0:T(1,128)S(1)} %copy.154, f32[3,3,258,1]{3,2,1,0:T(8,128)S(1)} %copy-done.5, ...), kind=kLoop, calls=%fused_computation.25 | loop fusion | flops 6193152 | bytes 8678544 | tf_op jit(solution)/shard_map/div | solution.py:63
  (52 shorter events, 0.2 us)
Async XLA Ops:
  0.0 2.5 %copy-start = (f32[3,3,256,128]{3,2,1,0:T(8,128)S(1)}, f32[3,3,256,128]{3,2,1,0:T(8,128)}, u32[]{:S(2)}) copy-start(f32[3,3,256,128]{3,2,1,0:T(8,128)} %param.10) | copy-start | bytes 3538948
  0.0 18.0 %copy-start.18 = (s32[256]{0:T(256)S(1)}, s32[256]{0:T(256)}, u32[]{:S(2)}) copy-start(s32[256]{0:T(256)} %param.16) | copy-start | bytes 3076
  0.0 18.0 %copy-start.17 = (f32[9,256]{1,0:T(8,128)S(1)}, f32[9,256]{1,0:T(8,128)}, u32[]{:S(2)}) copy-start(f32[9,256]{1,0:T(8,128)} %param.15) | copy-start | bytes 27652
  2.5 69.8 %collective-permute-start = (f32[3,3,1,128]{3,1,2,0:T(4,128)S(1)}, f32[3,3,1,128]{3,1,2,0:T(4,128)S(1)}, u32[]{:S(2)}, u32[]{:S(2)}) collective-permute-start(f32[3,3,1,128]{3,1,2,0:T(4,128)S(1)} %copy.164), channel_id=1, source_target_pairs={{16,0},{32,16},{48,32},{64,48},{80,64},{96,80},{112,96},{128,112},... | collective-permute-start | bytes 13832 | tf_op jit(solution)/shard_map/ppermute | solution.py:18
  15.4 56.9 %collective-permute-start.1 = (f32[3,3,1,128]{3,1,2,0:T(4,128)S(1)}, f32[3,3,1,128]{3,1,2,0:T(4,128)S(1)}, u32[]{:S(2)}, u32[]{:S(2)}) collective-permute-start(f32[3,3,1,128]{3,1,2,0:T(4,128)S(1)} %copy.165), channel_id=1, source_target_pairs={{0,16},{16,32},{32,48},{48,64},{64,80},{80,96},{96,112},{112,128},... | collective-permute-start | bytes 13832 | tf_op jit(solution)/shard_map/ppermute | solution.py:17
  68.9 2.7 %copy-start.15 = (f32[8]{0:T(128)S(1)}, f32[8]{0:T(128)}, u32[]{:S(2)}) copy-start(f32[8]{0:T(128)} %param.13) | copy-start | bytes 100
  73.9 19.3 %copy-start.16 = (f32[8]{0:T(128)S(1)}, f32[8]{0:T(128)}, u32[]{:S(2)}) copy-start(f32[8]{0:T(128)} %param.14) | copy-start | bytes 100
  73.9 20.0 %copy-start.14 = (s32[3,256,128]{2,1,0:T(8,128)S(1)}, s32[3,256,128]{2,1,0:T(8,128)}, u32[]{:S(2)}) copy-start(s32[3,256,128]{2,1,0:T(8,128)} %param.12) | copy-start | bytes 1179652
  75.9 25.3 %collective-permute-start.2 = (f32[3,3,258,1]{2,1,3,0:T(4,128)S(1)}, f32[3,3,258,1]{2,1,3,0:T(4,128)S(1)}, u32[]{:S(2)}, u32[]{:S(2)}) collective-permute-start(f32[3,3,258,1]{2,1,3,0:T(4,128)S(1)} %copy.136), channel_id=1, source_target_pairs={{1,0},{2,1},{3,2},{4,3},{5,4},{6,5},{7,6},{8,7},{9,8},{10,9},{11,1... | collective-permute-start | bytes 27872 | tf_op jit(solution)/shard_map/ppermute | solution.py:18
  96.9 33.2 %collective-permute-start.7 = (f32[3,3,258,1]{2,1,3,0:T(4,128)S(1)}, f32[3,3,258,1]{2,1,3,0:T(4,128)S(1)}, u32[]{:S(2)}, u32[]{:S(2)}) collective-permute-start(f32[3,3,258,1]{2,1,3,0:T(4,128)S(1)} %copy.144), channel_id=1, source_target_pairs={{0,1},{1,2},{2,3},{3,4},{4,5},{5,6},{6,7},{7,8},{8,9},{9,10},{10,1... | collective-permute-start | bytes 27872 | tf_op jit(solution)/shard_map/ppermute | solution.py:17
  103.3 20.9 %copy-start.3 = (f32[3,3,256,128]{3,2,1,0:T(8,128)S(1)}, f32[3,3,256,128]{3,2,1,0:T(8,128)}, u32[]{:S(2)}) copy-start(f32[3,3,256,128]{3,2,1,0:T(8,128)} %copy.169) | copy-start | bytes 3538948
  103.3 20.9 %copy-start.6 = (f32[3,3,256,1]{3,2,1,0:T(8,128)S(1)}, f32[3,3,256,1]{3,2,1,0:T(8,128)}, u32[]{:S(2)}) copy-start(f32[3,3,256,1]{3,2,1,0:T(8,128)} %reshape.66) | copy-start | bytes 27652
  116.8 14.8 %collective-permute-start.4 = (f32[1,3,1,128]{2,1,3,0:T(4,128)}, f32[1,3,1,128]{2,1,3,0:T(4,128)S(1)}, u32[]{:S(2)}, u32[]{:S(2)}) collective-permute-start(f32[1,3,1,128]{2,1,3,0:T(4,128)} %get-tuple-element.34), channel_id=1, source_target_pairs={{0,16},{16,32},{32,48},{48,64},{64,80},{80,96},{96,112},{112,128},... | collective-permute-start | bytes 4616 | tf_op jit(solution)/shard_map/ppermute | solution.py:17
  118.8 14.4 %collective-permute-start.3 = (f32[1,3,1,128]{2,1,3,0:T(4,128)}, f32[1,3,1,128]{2,1,3,0:T(4,128)S(1)}, u32[]{:S(2)}, u32[]{:S(2)}) collective-permute-start(f32[1,3,1,128]{2,1,3,0:T(4,128)} %get-tuple-element.35), channel_id=1, source_target_pairs={{16,0},{32,16},{48,32},{64,48},{80,64},{96,80},{112,96},{128,112},... | collective-permute-start | bytes 4616 | tf_op jit(solution)/shard_map/ppermute | solution.py:18
  133.2 11.2 %collective-permute-start.6 = (f32[1,3,258,1]{2,1,3,0:T(4,128)S(1)}, f32[1,3,258,1]{2,1,3,0:T(4,128)S(1)}, u32[]{:S(2)}, u32[]{:S(2)}) collective-permute-start(f32[1,3,258,1]{2,1,3,0:T(4,128)S(1)} %get-tuple-element.30), channel_id=1, source_target_pairs={{0,1},{1,2},{2,3},{3,4},{4,5},{5,6},{6,7},{7,8},{8,9},{9,10},{10,1... | collective-permute-start | bytes 9296 | tf_op jit(solution)/shard_map/ppermute | solution.py:17
  137.9 6.5 %collective-permute-start.5 = (f32[1,3,258,1]{2,1,3,0:T(4,128)S(1)}, f32[1,3,258,1]{2,1,3,0:T(4,128)S(1)}, u32[]{:S(2)}, u32[]{:S(2)}) collective-permute-start(f32[1,3,258,1]{2,1,3,0:T(4,128)S(1)} %get-tuple-element.31), channel_id=1, source_target_pairs={{1,0},{2,1},{3,2},{4,3},{5,4},{6,5},{7,6},{8,7},{9,8},{10,9},{11,1... | collective-permute-start | bytes 9296 | tf_op jit(solution)/shard_map/ppermute | solution.py:18
  158.2 6.0 %copy-start.7 = (f32[3,256,128]{2,1,0:T(8,128)S(1)}, f32[3,256,128]{2,1,0:T(8,128)}, u32[]{:S(2)}) copy-start(f32[3,256,128]{2,1,0:T(8,128)} %copy.142) | copy-start | bytes 1179652
  158.2 6.0 %copy-start.8 = (f32[3,256,128]{2,1,0:T(8,128)S(1)}, f32[3,256,128]{2,1,0:T(8,128)}, u32[]{:S(2)}) copy-start(f32[3,256,128]{2,1,0:T(8,128)} %copy.143) | copy-start | bytes 1179652
  169.1 8.6 %copy-start.1 = (f32[3,3,256,128]{3,2,1,0:T(8,128)}, f32[3,3,256,128]{3,2,1,0:T(8,128)S(1)}, u32[]{:S(2)}) copy-start(f32[3,3,256,128]{3,2,1,0:T(8,128)S(1)} %fusion.16) | copy-start | bytes 3538948
  169.1 5.3 %collective-permute-start.8 = (f32[3,3,1,128]{3,1,2,0:T(4,128)S(1)}, f32[3,3,1,128]{3,1,2,0:T(4,128)S(1)}, u32[]{:S(2)}, u32[]{:S(2)}) collective-permute-start(f32[3,3,1,128]{3,1,2,0:T(4,128)S(1)} %copy.151), channel_id=1, source_target_pairs={{16,0},{32,16},{48,32},{64,48},{80,64},{96,80},{112,96},{128,112},... | collective-permute-start | bytes 13832 | tf_op jit(solution)/shard_map/ppermute | solution.py:18
  171.1 6.5 %collective-permute-start.9 = (f32[3,3,1,128]{3,1,2,0:T(4,128)S(1)}, f32[3,3,1,128]{3,1,2,0:T(4,128)S(1)}, u32[]{:S(2)}, u32[]{:S(2)}) collective-permute-start(f32[3,3,1,128]{3,1,2,0:T(4,128)S(1)} %copy.153), channel_id=1, source_target_pairs={{0,16},{16,32},{32,48},{48,64},{64,80},{80,96},{96,112},{112,128},... | collective-permute-start | bytes 13832 | tf_op jit(solution)/shard_map/ppermute | solution.py:17
  181.1 9.8 %collective-permute-start.11 = (f32[3,3,258,1]{2,1,3,0:T(4,128)S(1)}, f32[3,3,258,1]{2,1,3,0:T(4,128)S(1)}, u32[]{:S(2)}, u32[]{:S(2)}) collective-permute-start(f32[3,3,258,1]{2,1,3,0:T(4,128)S(1)} %copy.159), channel_id=1, source_target_pairs={{0,1},{1,2},{2,3},{3,4},{4,5},{5,6},{6,7},{7,8},{8,9},{9,10},{10,1... | collective-permute-start | bytes 27872 | tf_op jit(solution)/shard_map/ppermute | solution.py:17
  188.8 8.2 %copy-start.2 = (f32[3,3,256,128]{3,2,1,0:T(8,128)S(1)}, f32[3,3,256,128]{3,2,1,0:T(8,128)}, u32[]{:S(2)}) copy-start(f32[3,3,256,128]{3,2,1,0:T(8,128)} %copy-done.1) | copy-start | bytes 3538948
  188.8 6.7 %collective-permute-start.10 = (f32[3,3,258,1]{2,1,3,0:T(4,128)S(1)}, f32[3,3,258,1]{2,1,3,0:T(4,128)S(1)}, u32[]{:S(2)}, u32[]{:S(2)}) collective-permute-start(f32[3,3,258,1]{2,1,3,0:T(4,128)S(1)} %copy.157), channel_id=1, source_target_pairs={{1,0},{2,1},{3,2},{4,3},{5,4},{6,5},{7,6},{8,7},{9,8},{10,9},{11,1... | collective-permute-start | bytes 27872 | tf_op jit(solution)/shard_map/ppermute | solution.py:18
  197.0 3.3 %copy-start.4 = (f32[3,3,256,128]{3,2,1,0:T(8,128)S(1)}, f32[3,3,256,128]{3,2,1,0:T(8,128)}, u32[]{:S(2)}) copy-start(f32[3,3,256,128]{3,2,1,0:T(8,128)} %scatter-add.4) | copy-start | bytes 3538948
  197.0 3.3 %copy-start.5 = (f32[3,3,258,1]{3,2,1,0:T(8,128)S(1)}, f32[3,3,258,1]{3,2,1,0:T(8,128)}, u32[]{:S(2)}) copy-start(f32[3,3,258,1]{3,2,1,0:T(8,128)} %copy.158) | copy-start | bytes 27868
  197.0 3.3 %copy-start.9 = (f32[3,256,128]{2,1,0:T(8,128)S(1)}, f32[3,256,128]{2,1,0:T(8,128)}, u32[]{:S(2)}) copy-start(f32[3,256,128]{2,1,0:T(8,128)} %copy.140) | copy-start | bytes 1179652
  197.0 3.4 %copy-start.10 = (f32[3,256,128]{2,1,0:T(8,128)S(1)}, f32[3,256,128]{2,1,0:T(8,128)}, u32[]{:S(2)}) copy-start(f32[3,256,128]{2,1,0:T(8,128)} %copy.146) | copy-start | bytes 1179652
  197.0 3.4 %copy-start.11 = (f32[3,256,128]{2,1,0:T(8,128)S(1)}, f32[3,256,128]{2,1,0:T(8,128)}, u32[]{:S(2)}) copy-start(f32[3,256,128]{2,1,0:T(8,128)} %copy.150) | copy-start | bytes 1179652
  197.0 3.4 %copy-start.12 = (f32[3,256,128]{2,1,0:T(8,128)S(1)}, f32[3,256,128]{2,1,0:T(8,128)}, u32[]{:S(2)}) copy-start(f32[3,256,128]{2,1,0:T(8,128)} %copy.149) | copy-start | bytes 1179652
  197.0 3.4 %copy-start.13 = (f32[3,256,128]{2,1,0:T(8,128)S(1)}, f32[3,256,128]{2,1,0:T(8,128)}, u32[]{:S(2)}) copy-start(f32[3,256,128]{2,1,0:T(8,128)} %copy.139) | copy-start | bytes 1179652
where the time goes:
time: 205 us; the launch traced here: 204 us
  starting transfers between devices  64.8 us (32%)
  blocking collectives  50.8 us (25%)
  local copies, waits for them, and re-layouts  38.9 us (19%)
  other arithmetic  36.6 us (18%)
  waiting for transfers between devices  8.85 us (4%)
  matrix products  2.68 us (1%)
    all_gather x1, blocking collectives, local(): lax.all_gather(packed, 'az', axis=1, tiled=True)  50.8 us
    ppermute x6, starting transfers between devices, with_halo(): after = lax.ppermute(first, axis, down)  41.7 us
    ppermute x6, starting transfers between devices, with_halo(): before = lax.ppermute(last, axis, up)  23.1 us
    mul x1, other arithmetic, local(): reluct = base_reluct * (1.0 + saturation * flux_sq / (1.0 + flux_sq))  12.6 us
    mul x6, local copies, waits for them, and re-layouts, jacobi_sweep(): face_coef * offset_view(padded_field, layer_step, az_step, rad_step)  11.9 us
    concatenate x6, other arithmetic, with_halo(): x = jnp.concatenate([before, x, after], axis=dim)  8.73 us
    div x2, other arithmetic, jacobi_sweep(): return numerator / denominator  8.29 us
    slice x8, local copies, waits for them, and re-layouts, with_halo(): last = lax.slice_in_dim(x, length - width, length, axis=dim)  6.5 us
  transfers between devices with their start and end apart: 12, of which 3 were waited for; matrix products, arithmetic and copies ran while one was open for 17% of the time, Pallas kernels for 0%

commit v1 on v0

v1 whole, which is shorter than its diff:
```python
import jax
import jax.numpy as jnp
from jax import lax
from jax.experimental import pallas as pl
from jax.experimental.pallas import tpu as pltpu
from jax.sharding import PartitionSpec as P

MESH = pl.DeviceIdType.MESH
F32 = jnp.float32
L, NF, MAT = 3, 9, 8
B = 16
LANES = 128
STRIP = 384
TO_LEFT, TO_RIGHT = 48, 40


def lookup(material, table):
    low, mid, high = [(material & bit) != 0 for bit in (1, 2, 4)]
    pairs = [jnp.where(low, table[2 * i + 1], table[2 * i]) for i in range(4)]
    quads = [jnp.where(mid, pairs[2 * i + 1], pairs[2 * i]) for i in range(2)]
    return jnp.where(high, quads[1], quads[0])


def half_reluct(material, flux_sq, nu_half, sat):
    return lookup(material, nu_half) * (1.0 + lookup(material, sat) * flux_sq / (1.0 + flux_sq))


def sweep(values, source, faces, inverse):
    total = source
    for face, value in zip(faces, values):
        if value is not None:
            total = total + face * value
    return total * inverse


def kernel(
    pot, cur, mat, nu, sat, flux, jitter, offset, out,
    a_ext, c_ext, m_ext, q_ext, inv_ext, v_ext,
    to_prev, to_next, from_prev, from_next,
    left_main, left_corner, right_main, right_corner,
    in_right_main, in_right_corner, in_left_main, in_left_corner,
    s_a, s_m, s_c, s_q, s_inv, s_v,
    block, land, acc, spread,
    load_sem, az_send, az_recv, rad_send, rad_recv, pan_send, pan_recv,
):
    az, rad = lax.axis_index("az"), lax.axis_index("rad")
    n_az, n_rad = lax.axis_size("az"), lax.axis_size("rad")
    n_z = n_az // 2
    rows = pot.shape[1]
    cells = rows * n_az
    z, x = az // 2, az % 2
    stator = n_rad // 2
    gap = (rad == stator) | (rad == stator - 1)
    has_left, has_right = rad > 0, rad < n_rad - 1
    reach_z = z + n_z // 2
    slot_k = reach_z % n_z
    direct = gap & (az != 0) & (slot_k >= 0) & ((slot_k < 6) | (slot_k > 10))

    def place(dz, dx):
        return (((z + dz + n_z) % n_z) * 2 + (x + dx) % 2, rad)

    loads = [
        pltpu.make_async_copy(pot, a_ext.at[:, pl.ds(B, rows), :], load_sem.at[0]),
        pltpu.make_async_copy(cur, c_ext.at[:, pl.ds(B, rows), :], load_sem.at[1]),
        pltpu.make_async_copy(mat, m_ext.at[:, pl.ds(B, rows), :], load_sem.at[2]),
    ]
    for load in loads:
        load.start()

    bar = pltpu.get_barrier_semaphore()
    prev, nxt = (az + n_az - 1) % n_az, (az + 1) % n_az

    def greet(who):
        pl.semaphore_signal(bar, inc=1, device_id=who, device_id_type=MESH)

    greet((prev, rad))
    greet((nxt, rad))

    @pl.when(has_left)
    def _():
        greet((az, rad - 1))

    @pl.when(has_right)
    def _():
        greet((az, rad + 1))

    window = [(dz, dx) for dz in (-2, -1, 0, 1, 2) for dx in (0, 1) if (dz, dx) != (0, 0)]

    @pl.when(gap)
    def _():
        for dz, dx in window:
            greet(place(dz, dx))

        @pl.when(az != 0)
        def _():
            greet(place(-3, 0))
            greet(place(3, 0))

        @pl.when(az == 0)
        def _():
            for far in range(3, n_z - 2):
                for side in (0, 1):
                    greet((far * 2 + side, rad))

    up_ok = jnp.logical_not((z == n_z - 3) & (x == 0))
    down_ok = jnp.logical_not((z == 3) & (x == 0))
    one = lambda flag: jnp.where(flag, 1, 0).astype(jnp.int32)
    expected = 2 + one(has_left) + one(has_right)
    expected = expected + one(gap) * (len(window) + one(up_ok) + one(down_ok)) + one(direct)

    half = rows // 2
    block[0:8, :] = flux[0:8, 0:half]
    block[8:16, :] = flux[0:8, half:rows]
    block[16:17, :] = flux[8:9, 0:half]
    block[17:18, :] = flux[8:9, half:rows]
    for part in (0, 1):
        turned = offset[0] + jitter[pl.ds(part * half, half)].reshape(1, half)
        turned = jnp.where(turned >= cells, turned - cells, turned)
        block[18 + part : 19 + part, :] = turned.astype(F32)
    block[20:24, :] = jnp.zeros((4, half), F32)

    for buf, count in ((a_ext, NF), (c_ext, NF), (m_ext, L)):
        for i in range(count):
            buf[i, 0:B, :] = jnp.zeros((B, LANES), buf.dtype)
            buf[i, B + rows : B + rows + B, :] = jnp.zeros((B, LANES), buf.dtype)

    pl.semaphore_wait(bar, expected)

    def panels(src, dst, send, recv, who):
        return pltpu.make_async_remote_copy(
            src_ref=src, dst_ref=dst, send_sem=pan_send.at[send], recv_sem=pan_recv.at[recv],
            device_id=who, device_id_type=MESH)

    def direct_copy(recv):
        return panels(block, land.at[slot_k * 2 + x], 9, recv, (0, rad))

    window_copies = [
        panels(block, land.at[(8 - dz) * 2 + x], i, 0, place(dz, dx)) for i, (dz, dx) in enumerate(window)
    ]
    own_copy = pltpu.make_async_copy(block, land.at[16 + x], pan_recv.at[0])
    far_regions = ((1, 3, 6), (2, 11, 14), (3, 0, 3), (4, 14, 16))

    @pl.when(gap)
    def _():
        for recv, low, high in far_regions:

            @pl.when(direct & (slot_k >= low) & (slot_k < high))
            def _():
                direct_copy(recv).start()

        for copy in window_copies:
            copy.start()
        own_copy.start()

    for load in loads:
        load.wait()
    last = B + rows
    for f in range(NF):
        to_prev[3 * f : 3 * f + 3, :] = a_ext[f, B : B + 3, :]
        to_prev[33 + f : 34 + f, :] = c_ext[f, B : B + 1, :]
        to_next[2 * f : 2 * f + 2, :] = a_ext[f, last - 2 : last, :]
        to_next[24 + f : 25 + f, :] = c_ext[f, last - 1 : last, :]
    for l in range(L):
        to_prev[27 + 2 * l : 29 + 2 * l, :] = m_ext[l, B : B + 2, :].astype(F32)
        to_next[18 + 2 * l : 20 + 2 * l, :] = m_ext[l, last - 2 : last, :].astype(F32)
    to_prev[42:48, :] = jnp.zeros((6, LANES), F32)
    to_next[33:40, :] = jnp.zeros((7, LANES), F32)

    def az_copy(src, dst, i, who):
        return pltpu.make_async_remote_copy(
            src_ref=src, dst_ref=dst, send_sem=az_send.at[i], recv_sem=az_recv.at[i],
            device_id=(who, rad), device_id_type=MESH)

    down_copy = az_copy(to_prev, from_next, 0, prev)
    up_copy = az_copy(to_next, from_prev, 1, nxt)
    down_copy.start()
    up_copy.start()

    def to_strip(f, dst, tile, lanes):
        turned = tile.T
        dst[f, 2:8, lanes] = turned[0:6]
        dst[f, 8:13, lanes] = turned[LANES - 5 : LANES]

    def pack(count, lanes, left, right):
        for f in range(NF):
            left[3 * f : 3 * f + 3, :] = s_a[f, 2:5, lanes]
            left[33 + f : 34 + f, :] = s_c[f, 2:3, lanes]
            right[2 * f : 2 * f + 2, :] = s_a[f, 11:13, lanes]
            right[24 + f : 25 + f, :] = s_c[f, 12:13, lanes]
        for l in range(L):
            left[27 + 2 * l : 29 + 2 * l, :] = s_m[l, 2:4, lanes]
            right[18 + 2 * l : 20 + 2 * l, :] = s_m[l, 11:13, lanes]
        left[42:48, :] = jnp.zeros((6, count), F32)
        right[33:40, :] = jnp.zeros((7, count), F32)

    def rad_copy(src, dst, i, who):
        return pltpu.make_async_remote_copy(
            src_ref=src, dst_ref=dst, send_sem=rad_send.at[i], recv_sem=rad_recv.at[i],
            device_id=(az, who), device_id_type=MESH)

    left_copies = (rad_copy(left_main, in_right_main, 0, rad - 1), rad_copy(left_corner, in_right_corner, 1, rad - 1))
    right_copies = (rad_copy(right_main, in_left_main, 2, rad + 1), rad_copy(right_corner, in_left_corner, 3, rad + 1))

    def send_strips(i):
        @pl.when(has_left)
        def _():
            left_copies[i].start()

        @pl.when(has_right)
        def _():
            right_copies[i].start()

    @pl.loop(0, NF)
    def _(f):
        for part in (0, 1):
            lanes = slice(part * LANES, (part + 1) * LANES)
            to_strip(f, s_a, a_ext[f, B + part * LANES : B + (part + 1) * LANES, :], lanes)
            to_strip(f, s_c, c_ext[f, B + part * LANES : B + (part + 1) * LANES, :], lanes)

    @pl.loop(0, L)
    def _(l):
        for part in (0, 1):
            lanes = slice(part * LANES, (part + 1) * LANES)
            to_strip(l, s_m, m_ext[l, B + part * LANES : B + (part + 1) * LANES, :].astype(F32), lanes)

    pack(rows, slice(0, rows), left_main, right_main)
    send_strips(0)

    down_copy.wait()
    up_copy.wait()
    for f in range(NF):
        a_ext[f, last : last + 3, :] = from_next[3 * f : 3 * f + 3, :]
        c_ext[f, last : last + 1, :] = from_next[33 + f : 34 + f, :]
        a_ext[f, B - 2 : B, :] = from_prev[2 * f : 2 * f + 2, :]
        c_ext[f, B - 1 : B, :] = from_prev[24 + f : 25 + f, :]
    for l in range(L):
        m_ext[l, last : last + 2, :] = from_next[27 + 2 * l : 29 + 2 * l, :].astype(jnp.int32)
        m_ext[l, B - 2 : B, :] = from_prev[18 + 2 * l : 20 + 2 * l, :].astype(jnp.int32)

    def rim(buf, f):
        gap_rows = jnp.zeros((LANES - 16, LANES), F32)
        return jnp.concatenate(
            [buf[f, last : last + 8, :].astype(F32), gap_rows, buf[f, B - 8 : B, :].astype(F32)], axis=0
        )

    ends = slice(rows, STRIP)

    @pl.loop(0, NF)
    def _(f):
        to_strip(f, s_a, rim(a_ext, f), ends)
        to_strip(f, s_c, rim(c_ext, f), ends)

    @pl.loop(0, L)
    def _(l):
        to_strip(l, s_m, rim(m_ext, l), ends)

    pack(LANES, ends, left_corner, right_corner)
    send_strips(1)

    nu_half = [nu[i] * 0.5 for i in range(MAT)]
    sat_of = [sat[i] for i in range(MAT)]

    @pl.loop(0, rows // 8 + 2)
    def _(i):
        e = pl.multiple_of(i * 8 + 8, 8)
        for l in range(L):
            flux_sq = jnp.zeros((8, LANES), F32)
            for c in range(3):
                here = a_ext[c * L + l, pl.ds(e, 8), :]
                along = a_ext[c * L + l, pl.ds(e + 1, 8), :] - here
                across = pltpu.roll(here, LANES - 1, 1) - here
                flux_sq = flux_sq + along * along + across * across
            q_ext[l, pl.ds(e, 8), :] = half_reluct(m_ext[l, pl.ds(e, 8), :], flux_sq, nu_half, sat_of)

    def region(low, high, recv):
        view = land.at[pl.ds(low, high - low)]
        return pltpu.make_async_copy(view, view, pan_recv.at[recv])

    two_up = panels(land.at[pl.ds(12, 6)], land.at[pl.ds(6, 6)], 10, 1, place(3, 0))
    two_down = panels(land.at[pl.ds(16, 6)], land.at[pl.ds(22, 6)], 11, 2, place(-3, 0))
    three_up = panels(land.at[pl.ds(6, 6)], land.at[pl.ds(0, 6)], 12, 3, place(3, 0))
    three_down = panels(land.at[pl.ds(22, 4)], land.at[pl.ds(28, 4)], 13, 4, place(-3, 0))

    def when_start(flag, copy):
        @pl.when(flag)
        def _():
            copy.start()

    @pl.when(gap)
    def _():
        region(12, 22, 0).wait()
        when_start(up_ok, two_up)
        when_start(down_ok, two_down)

    def faces_of(q, q_next, q_prev, q_right, q_left, q_above, q_below):
        faces = [q + q_next, q + q_prev, q + q_right, q + q_left]
        faces.append(q if q_above is None else q + q_above)
        faces.append(q if q_below is None else q + q_below)
        return faces

    def main_faces(e, l):
        q = q_ext[l, pl.ds(e, 8), :]
        return faces_of(
            q, q_ext[l, pl.ds(e + 1, 8), :], q_ext[l, pl.ds(e - 1, 8), :],
            pltpu.roll(q, LANES - 1, 1), pltpu.roll(q, 1, 1),
            q_ext[l + 1, pl.ds(e, 8), :] if l + 1 < L else None, q_ext[l - 1, pl.ds(e, 8), :] if l > 0 else None)

    def main_neighbours(field, e, c, l):
        here = field[c * L + l, pl.ds(e, 8), :]
        return [
            field[c * L + l, pl.ds(e + 1, 8), :], field[c * L + l, pl.ds(e - 1, 8), :],
            pltpu.roll(here, LANES - 1, 1), pltpu.roll(here, 1, 1),
            field[c * L + l + 1, pl.ds(e, 8), :] if l + 1 < L else None,
            field[c * L + l - 1, pl.ds(e, 8), :] if l > 0 else None]

    @pl.loop(0, rows // 8 + 2)
    def _(i):
        e = pl.multiple_of(i * 8 + 8, 8)
        for l in range(L):
            faces = main_faces(e, l)
            inverse = 1.0 / (1.0 + sum(faces[1:], faces[0]))
            inv_ext[l, pl.ds(e, 8), :] = inverse
            for c in range(3):
                source = c_ext[c * L + l, pl.ds(e, 8), :]
                v_ext[c * L + l, pl.ds(e, 8), :] = sweep(main_neighbours(a_ext, e, c, l), source, faces, inverse)

    @pl.when(gap)
    def _():
        region(6, 12, 1).wait()
        region(22, 28, 2).wait()
        when_start(up_ok, three_up)
        when_start(down_ok, three_down)

    @pl.loop(0, rows // 8)
    def _(i):
        e = pl.multiple_of(i * 8 + B, 8)
        for l in range(L):
            faces = main_faces(e, l)
            inverse = inv_ext[l, pl.ds(e, 8), :]
            for c in range(3):
                source = c_ext[c * L + l, pl.ds(e, 8), :]
                out[c * L + l, pl.ds(e - B, 8), :] = sweep(main_neighbours(v_ext, e, c, l), source, faces, inverse)

    for f in range(NF):
        s_c[f, 0:2, :] = jnp.zeros((2, STRIP), F32)
        s_c[f, 13:16, :] = jnp.zeros((3, STRIP), F32)
    for l in range(L):
        s_m[l, 15:16, :] = jnp.zeros((1, STRIP), F32)

    @pl.when(has_right)
    def _():
        for i, (came, lanes) in enumerate(((in_right_main, slice(0, rows)), (in_right_corner, ends))):
            rad_copy(left_main if i == 0 else left_corner, came, i, rad + 1).wait_recv()
            for f in range(NF):
                s_a[f, 13:16, lanes] = came[3 * f : 3 * f + 3, :]
                s_c[f, 13:14, lanes] = came[33 + f : 34 + f, :]
            for l in range(L):
                s_m[l, 13:15, lanes] = came[27 + 2 * l : 29 + 2 * l, :]

    @pl.when(has_left)
    def _():
        for i, (came, lanes) in enumerate(((in_left_main, slice(0, rows)), (in_left_corner, ends))):
            rad_copy(right_main if i == 0 else right_corner, came, i + 2, rad - 1).wait_recv()
            for f in range(NF):
                s_a[f, 0:2, lanes] = came[2 * f : 2 * f + 2, :]
                s_c[f, 1:2, lanes] = came[24 + f : 25 + f, :]
            for l in range(L):
                s_m[l, 0:2, lanes] = came[18 + 2 * l : 20 + 2 * l, :]

    @pl.when(jnp.logical_not(has_right))
    def _():
        for f in range(NF):
            s_a[f, 13:16, :] = jnp.zeros((3, STRIP), F32)
        for l in range(L):
            s_m[l, 13:15, :] = jnp.zeros((2, STRIP), F32)

    @pl.when(jnp.logical_not(has_left))
    def _():
        for f in range(NF):
            s_a[f, 0:2, :] = jnp.zeros((2, STRIP), F32)
        for l in range(L):
            s_m[l, 0:2, :] = jnp.zeros((2, STRIP), F32)

    column = lax.broadcasted_iota(jnp.int32, (16, STRIP), 0)
    outside = ((column < 2) & (rad == 0)) | ((column > 12) & (rad == n_rad - 1))
    after = lambda v: pltpu.roll(v, STRIP - 1, 1)
    before = lambda v: pltpu.roll(v, 1, 1)
    right_of = lambda v: pltpu.roll(v, 15, 0)
    left_of = lambda v: pltpu.roll(v, 1, 0)

    for l in range(L):
        flux_sq = jnp.zeros((16, STRIP), F32)
        for c in range(3):
            here = s_a[c * L + l]
            along, across = after(here) - here, right_of(here) - here
            flux_sq = flux_sq + along * along + across * across
        q = half_reluct(s_m[l].astype(jnp.int32), flux_sq, nu_half, sat_of)
        s_q[l] = jnp.where(outside, 0.0, q)

    def strip_faces(l):
        q = s_q[l]
        return faces_of(
            q, after(q), before(q), right_of(q), left_of(q),
            s_q[l + 1] if l + 1 < L else None, s_q[l - 1] if l > 0 else None)

    def strip_neighbours(field, c, l):
        here = field[c * L + l]
        return [
            after(here), before(here), right_of(here), left_of(here),
            field[c * L + l + 1] if l + 1 < L else None, field[c * L + l - 1] if l > 0 else None]

    for l in range(L):
        faces = strip_faces(l)
        inverse = 1.0 / (1.0 + sum(faces[1:], faces[0]))
        s_inv[l] = inverse
        for c in range(3):
            swept = sweep(strip_neighbours(s_a, c, l), s_c[c * L + l], faces, inverse)
            s_v[c * L + l] = jnp.where(outside, 0.0, swept)

    def deposit(low, high):
        @pl.loop(low, high)
        def _(slot):
            parts = []
            for part in (0, 1):
                cell = land[slot, 18 + part : 19 + part, :].astype(jnp.int32) - az * rows
                cell = jnp.where(cell < 0, cell + cells, cell)
                ahead = jnp.where(cell < rows + 8, cell, -1)
                cell = jnp.where(cell >= cells - 8, cell - (cells - 8) + rows + 8, ahead)
                places = lax.broadcasted_iota(jnp.int32, (rows + 16, half), 0)
                parts.append(jnp.where(places == cell, 1.0, 0.0).astype(jnp.bfloat16))
            onehot = jnp.concatenate(parts, axis=1)
            top = jnp.concatenate([land[slot, 0:8, :], land[slot, 8:16, :]], axis=1)
            ninth = jnp.concatenate([land[slot, 16:17, :], land[slot, 17:18, :]], axis=1)
            values = jnp.concatenate([top, ninth, jnp.zeros((7, rows), F32)], axis=0)
            first = values.astype(jnp.bfloat16)
            rest = values - first.astype(F32)
            second = rest.astype(jnp.bfloat16)
            third = (rest - second.astype(F32)).astype(jnp.bfloat16)
            terms = jnp.concatenate([first, second, third], axis=0)
            acc[...] += lax.dot_general(
                onehot, terms, (((1,), (1,)), ((), ())), preferred_element_type=F32
            )

    @pl.when(gap)
    def _():
        acc[...] = jnp.zeros_like(acc)
        spread[...] = jnp.zeros_like(spread)
        deposit(6, 28)
        region(0, 6, 3).wait()
        region(28, 32, 4).wait()
        deposit(0, 6)
        deposit(28, 32)
        spread[0 : rows + 8, 0:48] = acc[0 : rows + 8, :]
        spread[STRIP - 8 : STRIP, 0:48] = acc[rows + 8 : rows + 16, :]
        turned = jnp.concatenate(
            [spread[i * LANES : (i + 1) * LANES, :].T for i in range(3)], axis=1
        )
        airgap = turned[0:16] + turned[16:32] + turned[32:48]

        @pl.when(rad == stator)
        def _():
            for f in range(NF):
                row = airgap[f : f + 1]
                s_c[f, 2:3, :] = s_c[f, 2:3, :] + row
                s_v[f, 2:3, :] = s_v[f, 2:3, :] + row * s_inv[f % L, 2:3, :]

        @pl.when(rad == stator - 1)
        def _():
            for f in range(NF):
                s_v[f, 13:14, :] = s_v[f, 13:14, :] + airgap[f : f + 1] * s_inv[f % L, 13:14, :]

    lane = lax.broadcasted_iota(jnp.int32, (LANES, LANES), 1)
    edge = (lane < 2) | (lane > LANES - 4)
    for l in range(L):
        faces = strip_faces(l)
        for c in range(3):
            f = c * L + l
            done = sweep(strip_neighbours(s_v, c, l), s_c[f], faces, s_inv[l])
            for part in (0, 1):
                piece = done[:, part * LANES : (part + 1) * LANES]
                tall = jnp.concatenate([piece[2:10], jnp.zeros((LANES - 16, LANES), F32), piece[5:13]], axis=0)
                own = out[f, part * LANES : (part + 1) * LANES, :]
                out[f, part * LANES : (part + 1) * LANES, :] = jnp.where(edge, tall.T, own)

    for i in (0, 1):
        @pl.when(has_left)
        def _():
            left_copies[i].wait_send()

        @pl.when(has_right)
        def _():
            right_copies[i].wait_send()

    @pl.when(gap)
    def _():
        for copy in window_copies:
            copy.wait_send()

        @pl.when(direct)
        def _():
            direct_copy(1).wait_send()

        @pl.when(up_ok)
        def _():
            two_up.wait_send()
            three_up.wait_send()

        @pl.when(down_ok)
        def _():
            two_down.wait_send()
            three_down.wait_send()


def local(potential, current, material, nu_table, sat_table, panel_flux, panel_jitter, rotor_offset):
    rows, lanes = potential.shape[2:]
    vmem = lambda *shape: pltpu.VMEM(shape, F32)
    tall = rows + 2 * B
    any_spec = pl.BlockSpec(memory_space=pl.ANY)
    smem = pl.BlockSpec(memory_space=pltpu.SMEM)
    whole = pl.BlockSpec(memory_space=pltpu.VMEM)
    result = pl.pallas_call(
        kernel,
        out_shape=jax.ShapeDtypeStruct((NF, rows, lanes), F32),
        in_specs=[any_spec, any_spec, any_spec, smem, smem, whole, whole, smem],
        out_specs=whole,
        scratch_shapes=[
            vmem(NF, tall, lanes), vmem(NF, tall, lanes), pltpu.VMEM((L, tall, lanes), jnp.int32),
            vmem(L, tall, lanes), vmem(L, tall, lanes), vmem(NF, tall, lanes),
            vmem(TO_LEFT, lanes), vmem(TO_RIGHT, lanes), vmem(TO_RIGHT, lanes), vmem(TO_LEFT, lanes),
            vmem(TO_LEFT, rows), vmem(TO_LEFT, LANES), vmem(TO_RIGHT, rows), vmem(TO_RIGHT, LANES),
            vmem(TO_LEFT, rows), vmem(TO_LEFT, LANES), vmem(TO_RIGHT, rows), vmem(TO_RIGHT, LANES),
            vmem(NF, 16, STRIP), vmem(L, 16, STRIP), vmem(NF, 16, STRIP),
            vmem(L, 16, STRIP), vmem(L, 16, STRIP), vmem(NF, 16, STRIP),
            vmem(24, LANES), vmem(32, 24, LANES), vmem(rows + 16, 48), vmem(STRIP, LANES),
            pltpu.SemaphoreType.DMA((3,)), pltpu.SemaphoreType.DMA((2,)), pltpu.SemaphoreType.DMA((2,)),
            pltpu.SemaphoreType.DMA((4,)), pltpu.SemaphoreType.DMA((4,)),
            pltpu.SemaphoreType.DMA((14,)), pltpu.SemaphoreType.DMA((5,)),
        ],
        compiler_params=pltpu.CompilerParams(
            collective_id=0, has_side_effects=True, vmem_limit_bytes=48 * 1024 * 1024
        ),
    )(
        potential.reshape(NF, rows, lanes), current.reshape(NF, rows, lanes), material,
        nu_table, sat_table, panel_flux, panel_jitter, rotor_offset,
    )
    return result.reshape(potential.shape)


def solution(mesh):
    placed = (
        P(None, None, "az", "rad"),
        P(None, None, "az", "rad"),
        P(None, "az", "rad"),
        P(),
        P(),
        P(None, "az"),
        P("az"),
        P(),
    )
    return jax.shard_map(
        local, mesh=mesh, in_specs=placed, out_specs=P(None, None, "az", "rad"), check_vma=False
    )
```

time: 205 us -> 44.6 us (0.22)
  the two profiles are of different devices: /device:TPU:1 before, /device:TPU:48 now
where the time goes in v1:
time: 44.6 us; the launch traced here: 44.3 us
  Pallas kernels  36.4 us (82%)
  local copies, waits for them, and re-layouts  7.25 us (16%)
  between operations  0.67 us (2%)
    pallas_call x1, Pallas kernels, local(): pl.pallas_call(kernel, out_shape=jax.ShapeDtypeStruct((NF, rows, lanes),...  36.4 us
    unnamed x15, local copies, waits for them, and re-layouts  7.25 us

profile of v1, /device:TPU:48, one launch (start us, length us, event | category | flops | bytes accessed | tf_op | source)
XLA Modules:
  0.0 44.3 jit_solution(9335270257822402601)
XLA Ops:
  0.7 0.0 copy-start
  0.7 1.3 %copy-done = f32[3,3,256,128]{3,2,1,0:T(8,128)S(1)} copy-done((f32[3,3,256,128]{3,2,1,0:T(8,128)S(1)}, f32[3,3,256,128]{3,2,1,0:T(8,128)}, u32[]{:S(2)}) %copy-start) | copy-done | bytes 1179672
  1.9 0.0 copy-start.1
  1.9 1.3 %copy-done.1 = f32[3,3,256,128]{3,2,1,0:T(8,128)S(1)} copy-done((f32[3,3,256,128]{3,2,1,0:T(8,128)S(1)}, f32[3,3,256,128]{3,2,1,0:T(8,128)}, u32[]{:S(2)}) %copy-start.1) | copy-done | bytes 1179672
  3.2 0.0 copy-start.2
  3.2 1.0 %copy-done.2 = s32[3,256,128]{2,1,0:T(8,128)S(1)} copy-done((s32[3,256,128]{2,1,0:T(8,128)S(1)}, s32[3,256,128]{2,1,0:T(8,128)}, u32[]{:S(2)}) %copy-start.2) | copy-done | bytes 393240
  4.2 0.0 copy-start.3
  4.2 0.7 %copy-done.3 = f32[9,256]{1,0:T(8,128)S(1)} copy-done((f32[9,256]{1,0:T(8,128)S(1)}, f32[9,256]{1,0:T(8,128)}, u32[]{:S(2)}) %copy-start.3) | copy-done | bytes 9240
  4.9 0.0 copy-start.4
  4.9 0.7 %copy-done.4 = s32[256]{0:T(256)S(1)} copy-done((s32[256]{0:T(256)S(1)}, s32[256]{0:T(256)}, u32[]{:S(2)}) %copy-start.4) | copy-done | bytes 1048
  5.6 0.0 copy-start.5
  5.6 0.7 %copy-done.5 = f32[8]{0:T(128)S(1)} copy-done((f32[8]{0:T(128)S(1)}, f32[8]{0:T(128)}, u32[]{:S(2)}) %copy-start.5) | copy-done | bytes 56
  6.2 0.0 copy-start.6
  6.2 0.7 %copy-done.6 = f32[8]{0:T(128)S(1)} copy-done((f32[8]{0:T(128)S(1)}, f32[8]{0:T(128)}, u32[]{:S(2)}) %copy-start.6) | copy-done | bytes 56
  6.9 36.4 %shard_map.82 = f32[9,256,128]{2,1,0:T(8,128)S(1)} custom-call(f32[9,256,128]{2,1,0:T(8,128)S(1)} %bitcast.4, f32[9,256,128]{2,1,0:T(8,128)S(1)} %bitcast.5, s32[3,256,128]{2,1,0:T(8,128)S(1)} %copy-done.2, f32[8]{0:T(128)S(1)} %copy-done.5, f32[8]{0:T(128)S(1)} %copy-done.6, f32[9,256]{1,0:T(8,128)S(1)} %copy-done.3, s32[256]{0:T(256)S(1)} %copy-done.4, ...), custom_call_target="tpu_custom_call" | custom-call | tf_op jit(solution)/shard_map/pallas_call | solution.py:521
  43.3 1.0 %copy.11 = f32[3,3,256,128]{3,2,1,0:T(8,128)} copy(f32[3,3,256,128]{3,2,1,0:T(8,128)S(1)} %bitcast.3) | data formatting | bytes 2359296
Async XLA Ops:
  0.7 1.3 %copy-start = (f32[3,3,256,128]{3,2,1,0:T(8,128)S(1)}, f32[3,3,256,128]{3,2,1,0:T(8,128)}, u32[]{:S(2)}) copy-start(f32[3,3,256,128]{3,2,1,0:T(8,128)} %param.8) | copy-start | bytes 3538948
  1.9 1.3 %copy-start.1 = (f32[3,3,256,128]{3,2,1,0:T(8,128)S(1)}, f32[3,3,256,128]{3,2,1,0:T(8,128)}, u32[]{:S(2)}) copy-start(f32[3,3,256,128]{3,2,1,0:T(8,128)} %param.9) | copy-start | bytes 3538948
  3.2 1.0 %copy-start.2 = (s32[3,256,128]{2,1,0:T(8,128)S(1)}, s32[3,256,128]{2,1,0:T(8,128)}, u32[]{:S(2)}) copy-start(s32[3,256,128]{2,1,0:T(8,128)} %mat.1) | copy-start | bytes 1179652
  4.2 0.7 %copy-start.3 = (f32[9,256]{1,0:T(8,128)S(1)}, f32[9,256]{1,0:T(8,128)}, u32[]{:S(2)}) copy-start(f32[9,256]{1,0:T(8,128)} %flux.1) | copy-start | bytes 27652
  4.9 0.7 %copy-start.4 = (s32[256]{0:T(256)S(1)}, s32[256]{0:T(256)}, u32[]{:S(2)}) copy-start(s32[256]{0:T(256)} %jitter.1) | copy-start | bytes 3076
  5.6 0.7 %copy-start.5 = (f32[8]{0:T(128)S(1)}, f32[8]{0:T(128)}, u32[]{:S(2)}) copy-start(f32[8]{0:T(128)} %nu.1) | copy-start | bytes 100
  6.2 0.7 %copy-start.6 = (f32[8]{0:T(128)S(1)}, f32[8]{0:T(128)}, u32[]{:S(2)}) copy-start(f32[8]{0:T(128)} %sat.1) | copy-start | bytes 100

commit v2 on v1

--- a/solution.py
+++ b/solution.py
@@ -34,13 +34,14 @@
 
 
 def kernel(
-    pot, cur, mat, nu, sat, flux, jitter, offset, out,
+    pot, cur, mat, nu_hbm, sat_hbm, flux_hbm, jitter_hbm, offset, out,
+    nu, sat, flux, jitter,
     a_ext, c_ext, m_ext, q_ext, inv_ext, v_ext,
     to_prev, to_next, from_prev, from_next,
     left_main, left_corner, right_main, right_corner,
     in_right_main, in_right_corner, in_left_main, in_left_corner,
     s_a, s_m, s_c, s_q, s_inv, s_v,
-    block, land, acc, spread,
+    block, land, acc, spread, stacked,
     load_sem, az_send, az_recv, rad_send, rad_recv, pan_send, pan_recv,
 ):
     az, rad = lax.axis_index("az"), lax.axis_index("rad")
@@ -64,7 +65,12 @@
         pltpu.make_async_copy(cur, c_ext.at[:, pl.ds(B, rows), :], load_sem.at[1]),
         pltpu.make_async_copy(mat, m_ext.at[:, pl.ds(B, rows), :], load_sem.at[2]),
     ]
-    for load in loads:
+    small = [
+        pltpu.make_async_copy(src, dst, load_sem.at[3 + i])
+        for i, (src, dst) in enumerate(
+            ((flux_hbm, flux), (jitter_hbm, jitter), (nu_hbm, nu), (sat_hbm, sat)))
+    ]
+    for load in small + loads:
         load.start()
 
     bar = pltpu.get_barrier_semaphore()
@@ -108,6 +114,8 @@
     expected = 2 + one(has_left) + one(has_right)
     expected = expected + one(gap) * (len(window) + one(up_ok) + one(down_ok)) + one(direct)
 
+    for load in small:
+        load.wait()
     half = rows // 2
     block[0:8, :] = flux[0:8, 0:half]
     block[8:16, :] = flux[0:8, half:rows]
@@ -119,38 +127,18 @@
         block[18 + part : 19 + part, :] = turned.astype(F32)
     block[20:24, :] = jnp.zeros((4, half), F32)
 
+    stacked[...] = jnp.zeros_like(stacked)
+
     for buf, count in ((a_ext, NF), (c_ext, NF), (m_ext, L)):
         for i in range(count):
             buf[i, 0:B, :] = jnp.zeros((B, LANES), buf.dtype)
             buf[i, B + rows : B + rows + B, :] = jnp.zeros((B, LANES), buf.dtype)
 
-    pl.semaphore_wait(bar, expected)
-
-    def panels(src, dst, send, recv, who):
-        return pltpu.make_async_remote_copy(
-            src_ref=src, dst_ref=dst, send_sem=pan_send.at[send], recv_sem=pan_recv.at[recv],
-            device_id=who, device_id_type=MESH)
-
-    def direct_copy(recv):
-        return panels(block, land.at[slot_k * 2 + x], 9, recv, (0, rad))
-
-    window_copies = [
-        panels(block, land.at[(8 - dz) * 2 + x], i, 0, place(dz, dx)) for i, (dz, dx) in enumerate(window)
-    ]
-    own_copy = pltpu.make_async_copy(block, land.at[16 + x], pan_recv.at[0])
-    far_regions = ((1, 3, 6), (2, 11, 14), (3, 0, 3), (4, 14, 16))
-
-    @pl.when(gap)
-    def _():
-        for recv, low, high in far_regions:
-
-            @pl.when(direct & (slot_k >= low) & (slot_k < high))
-            def _():
-                direct_copy(recv).start()
-
-        for copy in window_copies:
-            copy.start()
-        own_copy.start()
+    for f in range(NF):
+        s_c[f, 0:2, :] = jnp.zeros((2, STRIP), F32)
+        s_c[f, 13:16, :] = jnp.zeros((3, STRIP), F32)
+    for l in range(L):
+        s_m[l, 15:16, :] = jnp.zeros((1, STRIP), F32)
 
     for load in loads:
         load.wait()
@@ -166,15 +154,89 @@
     to_prev[42:48, :] = jnp.zeros((6, LANES), F32)
     to_next[33:40, :] = jnp.zeros((7, LANES), F32)
 
-    def az_copy(src, dst, i, who):
-        return pltpu.make_async_remote_copy(
-            src_ref=src, dst_ref=dst, send_sem=az_send.at[i], recv_sem=az_recv.at[i],
-            device_id=(who, rad), device_id_type=MESH)
-
-    down_copy = az_copy(to_prev, from_next, 0, prev)
-    up_copy = az_copy(to_next, from_prev, 1, nxt)
-    down_copy.start()
-    up_copy.start()
+    nu_half = [nu[i] * 0.5 for i in range(MAT)]
+    sat_of = [sat[i] for i in range(MAT)]
+
+    def faces_of(q, q_next, q_prev, q_right, q_left, q_above, q_below):
+        faces = [q + q_next, q + q_prev, q + q_right, q + q_left]
+        faces.append(q if q_above is None else q + q_above)
+        faces.append(q if q_below is None else q + q_below)
+        return faces
+
+    def main_faces(e, n, l):
+        q = q_ext[l, pl.ds(e, n), :]
+        return faces_of(
+            q, q_ext[l, pl.ds(e + 1, n), :], q_ext[l, pl.ds(e - 1, n), :],
+            pltpu.roll(q, LANES - 1, 1), pltpu.roll(q, 1, 1),
+            q_ext[l + 1, pl.ds(e, n), :] if l + 1 < L else None, q_ext[l - 1, pl.ds(e, n), :] if l > 0 else None)
+
+    def main_neighbours(field, e, n, c, l):
+        here = field[c * L + l, pl.ds(e, n), :]
+        return [
+            field[c * L + l, pl.ds(e + 1, n), :], field[c * L + l, pl.ds(e - 1, n), :],
+            pltpu.roll(here, LANES - 1, 1), pltpu.roll(here, 1, 1),
+            field[c * L + l + 1, pl.ds(e, n), :] if l + 1 < L else None,
+            field[c * L + l - 1, pl.ds(e, n), :] if l > 0 else None]
+
+    def reluct_rows(e, n):
+        for l in range(L):
+            flux_sq = jnp.zeros((n, LANES), F32)
+            for c in range(3):
+                here = a_ext[c * L + l, pl.ds(e, n), :]
+                along = a_ext[c * L + l, pl.ds(e + 1, n), :] - here
+                across = pltpu.roll(here, LANES - 1, 1) - here
+                flux_sq = flux_sq + along * along + across * across
+            q_ext[l, pl.ds(e, n), :] = half_reluct(m_ext[l, pl.ds(e, n), :], flux_sq, nu_half, sat_of)
+
+    def first_rows(e, n):
+        for l in range(L):
+            faces = main_faces(e, n, l)
+            inverse = 1.0 / (1.0 + sum(faces[1:], faces[0]))
+            inv_ext[l, pl.ds(e, n), :] = inverse
+            for c in range(3):
+                source = c_ext[c * L + l, pl.ds(e, n), :]
+                v_ext[c * L + l, pl.ds(e, n), :] = sweep(main_neighbours(a_ext, e, n, c, l), source, faces, inverse)
+
+    def second_rows(e, n):
+        for l in range(L):
+            faces = main_faces(e, n, l)
+            inverse = inv_ext[l, pl.ds(e, n), :]
+            for c in range(3):
+                source = c_ext[c * L + l, pl.ds(e, n), :]
+                out[c * L + l, pl.ds(e - B, n), :] = sweep(main_neighbours(v_ext, e, n, c, l), source, faces, inverse)
+
+    def outer(step, low, high):
+        (low_from, low_to), (high_from, high_to) = low, high
+        count_low, count = (low_to - low_from) // 8, (low_to - low_from + high_to - high_from) // 8
+
+        @pl.loop(0, count)
+        def _(i):
+            jump = jnp.where(i >= count_low, high_from - low_to, 0)
+            step(pl.multiple_of(low_from + i * 8 + jump, 8), 8)
+
+    def reluct_inner():
+        @pl.loop(0, rows // 16 - 1)
+        def _(i):
+            reluct_rows(pl.multiple_of(i * 16 + B, 16), 16)
+
+    def reluct_outer():
+        outer(reluct_rows, (B - 8, B), (last - 16, last + 8))
+
+    def first_outer():
+        outer(first_rows, (B - 8, B + 16), (last - 32, last + 8))
+
+    def second_outer():
+        outer(second_rows, (B, B + 32), (last - 48, last))
+
+    def first_inner():
+        @pl.loop(0, rows // 16 - 3)
+        def _(i):
+            first_rows(pl.multiple_of(i * 16 + B + 16, 16), 16)
+
+    def second_inner():
+        @pl.loop(0, rows // 16 - 5)
+        def _(i):
+            second_rows(pl.multiple_of(i * 16 + B + 32, 16), 16)
 
     def to_strip(f, dst, tile, lanes):
         turned = tile.T
@@ -193,6 +255,69 @@
         left[42:48, :] = jnp.zeros((6, count), F32)
         right[33:40, :] = jnp.zeros((7, count), F32)
 
+    def columns():
+        @pl.loop(0, NF)
+        def _(f):
+            for part in (0, 1):
+                lanes = slice(part * LANES, (part + 1) * LANES)
+                to_strip(f, s_a, a_ext[f, B + part * LANES : B + (part + 1) * LANES, :], lanes)
+                to_strip(f, s_c, c_ext[f, B + part * LANES : B + (part + 1) * LANES, :], lanes)
+
+        @pl.loop(0, L)
+        def _(l):
+            for part in (0, 1):
+                lanes = slice(part * LANES, (part + 1) * LANES)
+                to_strip(l, s_m, m_ext[l, B + part * LANES : B + (part + 1) * LANES, :].astype(F32), lanes)
+
+        pack(rows, slice(0, rows), left_main, right_main)
+
+    early = az == 0
+
+    @pl.when(early)
+    def _():
+        columns()
+        reluct_inner()
+        first_inner()
+        second_inner()
+
+    pl.semaphore_wait(bar, expected)
+
+    def panels(src, dst, send, recv, who):
+        return pltpu.make_async_remote_copy(
+            src_ref=src, dst_ref=dst, send_sem=pan_send.at[send], recv_sem=pan_recv.at[recv],
+            device_id=who, device_id_type=MESH)
+
+    def direct_copy(recv):
+        return panels(block, land.at[slot_k * 2 + x], 9, recv, (0, rad))
+
+    window_copies = [
+        panels(block, land.at[(8 - dz) * 2 + x], i, 0, place(dz, dx)) for i, (dz, dx) in enumerate(window)
+    ]
+    own_copy = pltpu.make_async_copy(block, land.at[16 + x], pan_recv.at[0])
+    far_regions = ((1, 3, 6), (2, 11, 14), (3, 0, 3), (4, 14, 16))
+
+    @pl.when(gap)
+    def _():
+        for recv, low, high in far_regions:
+
+            @pl.when(direct & (slot_k >= low) & (slot_k < high))
+            def _():
+                direct_copy(recv).start()
+
+        for copy in window_copies:
+            copy.start()
+        own_copy.start()
+
+    def az_copy(src, dst, i, who):
+        return pltpu.make_async_remote_copy(
+            src_ref=src, dst_ref=dst, send_sem=az_send.at[i], recv_sem=az_recv.at[i],
+            device_id=(who, rad), device_id_type=MESH)
+
+    down_copy = az_copy(to_prev, from_next, 0, prev)
+    up_copy = az_copy(to_next, from_prev, 1, nxt)
+    down_copy.start()
+    up_copy.start()
+
     def rad_copy(src, dst, i, who):
         return pltpu.make_async_remote_copy(
             src_ref=src, dst_ref=dst, send_sem=rad_send.at[i], recv_sem=rad_recv.at[i],
@@ -210,20 +335,10 @@
         def _():
             right_copies[i].start()
 
-    @pl.loop(0, NF)
-    def _(f):
-        for part in (0, 1):
-            lanes = slice(part * LANES, (part + 1) * LANES)
-            to_strip(f, s_a, a_ext[f, B + part * LANES : B + (part + 1) * LANES, :], lanes)
-            to_strip(f, s_c, c_ext[f, B + part * LANES : B + (part + 1) * LANES, :], lanes)
-
-    @pl.loop(0, L)
-    def _(l):
-        for part in (0, 1):
-            lanes = slice(part * LANES, (part + 1) * LANES)
-            to_strip(l, s_m, m_ext[l, B + part * LANES : B + (part + 1) * LANES, :].astype(F32), lanes)
-
-    pack(rows, slice(0, rows), left_main, right_main)
+    @pl.when(jnp.logical_not(early))
+    def _():
+        columns()
+
     send_strips(0)
 
     down_copy.wait()
@@ -237,40 +352,23 @@
         m_ext[l, last : last + 2, :] = from_next[27 + 2 * l : 29 + 2 * l, :].astype(jnp.int32)
         m_ext[l, B - 2 : B, :] = from_prev[18 + 2 * l : 20 + 2 * l, :].astype(jnp.int32)
 
-    def rim(buf, f):
-        gap_rows = jnp.zeros((LANES - 16, LANES), F32)
-        return jnp.concatenate(
-            [buf[f, last : last + 8, :].astype(F32), gap_rows, buf[f, B - 8 : B, :].astype(F32)], axis=0
-        )
-
     ends = slice(rows, STRIP)
-
-    @pl.loop(0, NF)
-    def _(f):
-        to_strip(f, s_a, rim(a_ext, f), ends)
-        to_strip(f, s_c, rim(c_ext, f), ends)
-
-    @pl.loop(0, L)
-    def _(l):
-        to_strip(l, s_m, rim(m_ext, l), ends)
+    fields = [(a_ext, s_a, f) for f in range(NF)] + [(c_ext, s_c, f) for f in range(NF)] + [(m_ext, s_m, l) for l in range(L)]
+    for low in range(0, len(fields), 8):
+        some = fields[low : low + 8]
+        stack = []
+        for buf, _, f in some:
+            stack += [buf[f, B - 8 : B, :].astype(F32), buf[f, last : last + 8, :].astype(F32)]
+        if len(some) < 8:
+            stack.append(jnp.zeros((LANES - 16 * len(some), LANES), F32))
+        turned = jnp.concatenate(stack, axis=0).T
+        for place_in, (_, dst, f) in enumerate(some):
+            shift = (LANES - 8 - 16 * place_in) % LANES
+            dst[f, 2:8, ends] = pltpu.roll(turned[0:8], shift, 1)[0:6]
+            dst[f, 8:13, ends] = pltpu.roll(turned[LANES - 8 : LANES], shift, 1)[3:8]
 
     pack(LANES, ends, left_corner, right_corner)
     send_strips(1)
-
-    nu_half = [nu[i] * 0.5 for i in range(MAT)]
-    sat_of = [sat[i] for i in range(MAT)]
-
-    @pl.loop(0, rows // 8 + 2)
-    def _(i):
-        e = pl.multiple_of(i * 8 + 8, 8)
-        for l in range(L):
-            flux_sq = jnp.zeros((8, LANES), F32)
-            for c in range(3):
-                here = a_ext[c * L + l, pl.ds(e, 8), :]
-                along = a_ext[c * L + l, pl.ds(e + 1, 8), :] - here
-                across = pltpu.roll(here, LANES - 1, 1) - here
-                flux_sq = flux_sq + along * along + across * across
-            q_ext[l, pl.ds(e, 8), :] = half_reluct(m_ext[l, pl.ds(e, 8), :], flux_sq, nu_half, sat_of)
 
     def region(low, high, recv):
         view = land.at[pl.ds(low, high - low)]
@@ -292,37 +390,15 @@
         when_start(up_ok, two_up)
         when_start(down_ok, two_down)
 
-    def faces_of(q, q_next, q_prev, q_right, q_left, q_above, q_below):
-        faces = [q + q_next, q + q_prev, q + q_right, q + q_left]
-        faces.append(q if q_above is None else q + q_above)
-        faces.append(q if q_below is None else q + q_below)
-        return faces
-
-    def main_faces(e, l):
-        q = q_ext[l, pl.ds(e, 8), :]
-        return faces_of(
-            q, q_ext[l, pl.ds(e + 1, 8), :], q_ext[l, pl.ds(e - 1, 8), :],
-            pltpu.roll(q, LANES - 1, 1), pltpu.roll(q, 1, 1),
-            q_ext[l + 1, pl.ds(e, 8), :] if l + 1 < L else None, q_ext[l - 1, pl.ds(e, 8), :] if l > 0 else None)
-
-    def main_neighbours(field, e, c, l):
-        here = field[c * L + l, pl.ds(e, 8), :]
-        return [
-            field[c * L + l, pl.ds(e + 1, 8), :], field[c * L + l, pl.ds(e - 1, 8), :],
-            pltpu.roll(here, LANES - 1, 1), pltpu.roll(here, 1, 1),
-            field[c * L + l + 1, pl.ds(e, 8), :] if l + 1 < L else None,
-            field[c * L + l - 1, pl.ds(e, 8), :] if l > 0 else None]
-
-    @pl.loop(0, rows // 8 + 2)
-    def _(i):
-        e = pl.multiple_of(i * 8 + 8, 8)
-        for l in range(L):
-            faces = main_faces(e, l)
-            inverse = 1.0 / (1.0 + sum(faces[1:], faces[0]))
-            inv_ext[l, pl.ds(e, 8), :] = inverse
-            for c in range(3):
-                source = c_ext[c * L + l, pl.ds(e, 8), :]
-                v_ext[c * L + l, pl.ds(e, 8), :] = sweep(main_neighbours(a_ext, e, c, l), source, faces, inverse)
+    late = jnp.logical_not(early)
+
+    @pl.when(late)
+    def _():
+        reluct_inner()
+        first_inner()
+
+    reluct_outer()
+    first_outer()
 
     @pl.when(gap)
     def _():
@@ -331,21 +407,41 @@
         when_start(up_ok, three_up)
         when_start(down_ok, three_down)
 
-    @pl.loop(0, rows // 8)
-    def _(i):
-        e = pl.multiple_of(i * 8 + B, 8)
-        for l in range(L):
-            faces = main_faces(e, l)
-            inverse = inv_ext[l, pl.ds(e, 8), :]
-            for c in range(3):
-                source = c_ext[c * L + l, pl.ds(e, 8), :]
-                out[c * L + l, pl.ds(e - B, 8), :] = sweep(main_neighbours(v_ext, e, c, l), source, faces, inverse)
-
-    for f in range(NF):
-        s_c[f, 0:2, :] = jnp.zeros((2, STRIP), F32)
-        s_c[f, 13:16, :] = jnp.zeros((3, STRIP), F32)
-    for l in range(L):
-        s_m[l, 15:16, :] = jnp.zeros((1, STRIP), F32)
+    @pl.when(late)
+    def _():
+        second_inner()
+
+    second_outer()
+
+    def deposit(low, high):
+        @pl.loop(low // 2, high // 2)
+        def _(pair):
+            hits, values = [], []
+            for slot in (2 * pair, 2 * pair + 1):
+                for part in (0, 1):
+                    cell = land[slot, 18 + part : 19 + part, :].astype(jnp.int32) - az * rows
+                    cell = jnp.where(cell < 0, cell + cells, cell)
+                    ahead = jnp.where(cell < rows + 8, cell, -1)
+                    cell = jnp.where(cell >= cells - 8, cell - (cells - 8) + rows + 8, ahead)
+                    places = lax.broadcasted_iota(jnp.int32, (rows + 16, half), 0)
+                    hits.append(jnp.where(places == cell, 1.0, 0.0).astype(jnp.bfloat16))
+                    ninth = land[slot, 16 + part : 17 + part, :]
+                    values.append(jnp.concatenate(
+                        [land[slot, 8 * part : 8 * part + 8, :], ninth, jnp.zeros((7, half), F32)], axis=0))
+            value = jnp.concatenate(values, axis=1)
+            first = value.astype(jnp.bfloat16)
+            rest = value - first.astype(F32)
+            second = rest.astype(jnp.bfloat16)
+            third = (rest - second.astype(F32)).astype(jnp.bfloat16)
+            acc[...] += lax.dot_general(
+                jnp.concatenate(hits, axis=1), jnp.concatenate([first, second, third], axis=0),
+                (((1,), (1,)), ((), ())), preferred_element_type=F32)
+
+    @pl.when(gap)
+    def _():
+        acc[...] = jnp.zeros_like(acc)
+        spread[...] = jnp.zeros_like(spread)
+        deposit(6, 28)
 
     @pl.when(has_right)
     def _():
@@ -417,35 +513,8 @@
             swept = sweep(strip_neighbours(s_a, c, l), s_c[c * L + l], faces, inverse)
             s_v[c * L + l] = jnp.where(outside, 0.0, swept)
 
-    def deposit(low, high):
-        @pl.loop(low, high)
-        def _(slot):
-            parts = []
-            for part in (0, 1):
-                cell = land[slot, 18 + part : 19 + part, :].astype(jnp.int32) - az * rows
-                cell = jnp.where(cell < 0, cell + cells, cell)
-                ahead = jnp.where(cell < rows + 8, cell, -1)
-                cell = jnp.where(cell >= cells - 8, cell - (cells - 8) + rows + 8, ahead)
-                places = lax.broadcasted_iota(jnp.int32, (rows + 16, half), 0)
-                parts.append(jnp.where(places == cell, 1.0, 0.0).astype(jnp.bfloat16))
-            onehot = jnp.concatenate(parts, axis=1)
-            top = jnp.concatenate([land[slot, 0:8, :], land[slot, 8:16, :]], axis=1)
-            ninth = jnp.concatenate([land[slot, 16:17, :], land[slot, 17:18, :]], axis=1)
-            values = jnp.concatenate([top, ninth, jnp.zeros((7, rows), F32)], axis=0)
-            first = values.astype(jnp.bfloat16)
-            rest = values - first.astype(F32)
-            second = rest.astype(jnp.bfloat16)
-            third = (rest - second.astype(F32)).astype(jnp.bfloat16)
-            terms = jnp.concatenate([first, second, third], axis=0)
-            acc[...] += lax.dot_general(
-                onehot, terms, (((1,), (1,)), ((), ())), preferred_element_type=F32
-            )
-
     @pl.when(gap)
     def _():
-        acc[...] = jnp.zeros_like(acc)
-        spread[...] = jnp.zeros_like(spread)
-        deposit(6, 28)
         region(0, 6, 3).wait()
         region(28, 32, 4).wait()
         deposit(0, 6)
@@ -476,11 +545,13 @@
         for c in range(3):
             f = c * L + l
             done = sweep(strip_neighbours(s_v, c, l), s_c[f], faces, s_inv[l])
-            for part in (0, 1):
-                piece = done[:, part * LANES : (part + 1) * LANES]
-                tall = jnp.concatenate([piece[2:10], jnp.zeros((LANES - 16, LANES), F32), piece[5:13]], axis=0)
-                own = out[f, part * LANES : (part + 1) * LANES, :]
-                out[f, part * LANES : (part + 1) * LANES, :] = jnp.where(edge, tall.T, own)
+            stacked[8 * f : 8 * f + 3, :] = done[10:13, 0:rows]
+            stacked[8 * f + 3 : 8 * f + 5, :] = done[2:4, 0:rows]
+    for part in (0, 1):
+        here = slice(part * LANES, (part + 1) * LANES)
+        turned = stacked[:, here].T
+        for f in range(NF):
+            out[f, here, :] = jnp.where(edge, pltpu.roll(turned, (LANES - 3 - 8 * f) % LANES, 1), out[f, here, :])
 
     for i in (0, 1):
         @pl.when(has_left)
@@ -515,15 +586,16 @@
     rows, lanes = potential.shape[2:]
     vmem = lambda *shape: pltpu.VMEM(shape, F32)
     tall = rows + 2 * B
-    any_spec = pl.BlockSpec(memory_space=pl.ANY)
-    smem = pl.BlockSpec(memory_space=pltpu.SMEM)
+    hbm = pl.BlockSpec(memory_space=pltpu.HBM)
     whole = pl.BlockSpec(memory_space=pltpu.VMEM)
     result = pl.pallas_call(
         kernel,
         out_shape=jax.ShapeDtypeStruct((NF, rows, lanes), F32),
-        in_specs=[any_spec, any_spec, any_spec, smem, smem, whole, whole, smem],
+        in_specs=[hbm] * 7 + [pl.BlockSpec(memory_space=pltpu.SMEM)],
         out_specs=whole,
         scratch_shapes=[
+            pltpu.SMEM((MAT,), F32), pltpu.SMEM((MAT,), F32), vmem(*panel_flux.shape),
+            pltpu.VMEM(panel_jitter.shape, jnp.int32),
             vmem(NF, tall, lanes), vmem(NF, tall, lanes), pltpu.VMEM((L, tall, lanes), jnp.int32),
             vmem(L, tall, lanes), vmem(L, tall, lanes), vmem(NF, tall, lanes),
             vmem(TO_LEFT, lanes), vmem(TO_RIGHT, lanes), vmem(TO_RIGHT, lanes), vmem(TO_LEFT, lanes),
@@ -531,8 +603,8 @@
             vmem(TO_LEFT, rows), vmem(TO_LEFT, LANES), vmem(TO_RIGHT, rows), vmem(TO_RIGHT, LANES),
             vmem(NF, 16, STRIP), vmem(L, 16, STRIP), vmem(NF, 16, STRIP),
             vmem(L, 16, STRIP), vmem(L, 16, STRIP), vmem(NF, 16, STRIP),
-            vmem(24, LANES), vmem(32, 24, LANES), vmem(rows + 16, 48), vmem(STRIP, LANES),
-            pltpu.SemaphoreType.DMA((3,)), pltpu.SemaphoreType.DMA((2,)), pltpu.SemaphoreType.DMA((2,)),
+            vmem(24, LANES), vmem(32, 24, LANES), vmem(rows + 16, 48), vmem(STRIP, LANES), vmem(LANES, rows),
+            pltpu.SemaphoreType.DMA((7,)), pltpu.SemaphoreType.DMA((2,)), pltpu.SemaphoreType.DMA((2,)),
             pltpu.SemaphoreType.DMA((4,)), pltpu.SemaphoreType.DMA((4,)),
             pltpu.SemaphoreType.DMA((14,)), pltpu.SemaphoreType.DMA((5,)),
         ],
@@ -540,8 +612,13 @@
             collective_id=0, has_side_effects=True, vmem_limit_bytes=48 * 1024 * 1024
         ),
     )(
-        potential.reshape(NF, rows, lanes), current.reshape(NF, rows, lanes), material,
-        nu_table, sat_table, panel_flux, panel_jitter, rotor_offset,
+        *[
+            pltpu.with_memory_space_constraint(v, pltpu.HBM)
+            for v in (
+                potential.reshape(NF, rows, lanes), current.reshape(NF, rows, lanes), material,
+                nu_table, sat_table, panel_flux, panel_jitter)
+        ],
+        rotor_offset,
     )
     return result.reshape(potential.shape)
 

time: 44.6 us -> 33.2 us (0.74)
  the two profiles are of different devices: /device:TPU:48 before, /device:TPU:18 now
where the time goes in v2:
time: 33.2 us; the launch traced here: 33.1 us
  Pallas kernels  31.4 us (95%)
  local copies, waits for them, and re-layouts  1.02 us (3%)
  between operations  0.66 us (2%)
    pallas_call x1, Pallas kernels, local(): pl.pallas_call(kernel, out_shape=jax.ShapeDtypeStruct((NF, rows, lanes),...  31.4 us
    unnamed x1, local copies, waits for them, and re-layouts  1.02 us

profile of v2, /device:TPU:18, one launch (start us, length us, event | category | flops | bytes accessed | tf_op | source)
XLA Modules:
  0.0 33.1 jit_solution(16103368604090957218)
XLA Ops:
  0.7 31.4 %shard_map.82 = f32[9,256,128]{2,1,0:T(8,128)S(1)} custom-call(f32[9,256,128]{2,1,0:T(8,128)} %bitcast.4, f32[9,256,128]{2,1,0:T(8,128)} %bitcast.5, s32[3,256,128]{2,1,0:T(8,128)} %mat.1, f32[8]{0:T(128)} %nu_hbm.1, f32[8]{0:T(128)} %sat_hbm.1, f32[9,256]{1,0:T(8,128)} %flux_hbm.1, s32[256]{0:T(256)} %jitter_hbm.1, s32[1]{0:T(128)S(6)} %copy.10.offset), custom_call_target="tpu_custom_call" | custom-call | tf_op jit(solution)/shard_map/pallas_call | solution.py:591
  32.0 1.0 %copy.11 = f32[3,3,256,128]{3,2,1,0:T(8,128)} copy(f32[3,3,256,128]{3,2,1,0:T(8,128)S(1)} %bitcast.3) | data formatting | bytes 2359296

commit v3 on v2

--- a/solution.py
+++ b/solution.py
@@ -8,6 +8,7 @@
 MESH = pl.DeviceIdType.MESH
 F32 = jnp.float32
 L, NF, MAT = 3, 9, 8
+SERVED = 1
 B = 16
 LANES = 128
 STRIP = 384
@@ -41,7 +42,7 @@
     left_main, left_corner, right_main, right_corner,
     in_right_main, in_right_corner, in_left_main, in_left_corner,
     s_a, s_m, s_c, s_q, s_inv, s_v,
-    block, land, acc, spread, stacked,
+    block, land, acc, spread, stacked, part_out, part_in,
     load_sem, az_send, az_recv, rad_send, rad_recv, pan_send, pan_recv,
 ):
     az, rad = lax.axis_index("az"), lax.axis_index("rad")
@@ -53,9 +54,9 @@
     stator = n_rad // 2
     gap = (rad == stator) | (rad == stator - 1)
     has_left, has_right = rad > 0, rad < n_rad - 1
-    reach_z = z + n_z // 2
-    slot_k = reach_z % n_z
-    direct = gap & (az != 0) & (slot_k >= 0) & ((slot_k < 6) | (slot_k > 10))
+    served = [(z_to, x_to) for z_to in range(SERVED) for x_to in (0, 1)]
+    slots = [(z - z_to + n_z // 2 + n_z) % n_z for z_to, _ in served]
+    direct = [gap & ((k < 6) | (k > 10)) for k in slots]
 
     def place(dz, dx):
         return (((z + dz + n_z) % n_z) * 2 + (x + dx) % 2, rad)
@@ -97,22 +98,22 @@
         for dz, dx in window:
             greet(place(dz, dx))
 
-        @pl.when(az != 0)
+        @pl.when(z >= SERVED)
         def _():
             greet(place(-3, 0))
             greet(place(3, 0))
 
-        @pl.when(az == 0)
+        @pl.when(z < SERVED)
         def _():
             for far in range(3, n_z - 2):
                 for side in (0, 1):
-                    greet((far * 2 + side, rad))
-
-    up_ok = jnp.logical_not((z == n_z - 3) & (x == 0))
-    down_ok = jnp.logical_not((z == 3) & (x == 0))
+                    greet((((z + far) % n_z) * 2 + side, rad))
+
+    up_ok = (z + 3) % n_z >= SERVED
+    down_ok = (z + n_z - 3) % n_z >= SERVED
     one = lambda flag: jnp.where(flag, 1, 0).astype(jnp.int32)
     expected = 2 + one(has_left) + one(has_right)
-    expected = expected + one(gap) * (len(window) + one(up_ok) + one(down_ok)) + one(direct)
+    expected = expected + one(gap) * (len(window) + one(up_ok) + one(down_ok)) + sum(one(flag) for flag in direct)
 
     for load in small:
         load.wait()
@@ -125,9 +126,9 @@
         turned = offset[0] + jitter[pl.ds(part * half, half)].reshape(1, half)
         turned = jnp.where(turned >= cells, turned - cells, turned)
         block[18 + part : 19 + part, :] = turned.astype(F32)
-    block[20:24, :] = jnp.zeros((4, half), F32)
 
     stacked[...] = jnp.zeros_like(stacked)
+    spread[...] = jnp.zeros_like(spread)
 
     for buf, count in ((a_ext, NF), (c_ext, NF), (m_ext, L)):
         for i in range(count):
@@ -271,7 +272,7 @@
 
         pack(rows, slice(0, rows), left_main, right_main)
 
-    early = az == 0
+    early = (gap & (z < 4)) | (az == 0)
 
     @pl.when(early)
     def _():
@@ -287,8 +288,9 @@
             src_ref=src, dst_ref=dst, send_sem=pan_send.at[send], recv_sem=pan_recv.at[recv],
             device_id=who, device_id_type=MESH)
 
-    def direct_copy(recv):
-        return panels(block, land.at[slot_k * 2 + x], 9, recv, (0, rad))
+    def direct_copy(i, recv):
+        z_to, x_to = served[i]
+        return panels(block, land.at[slots[i] * 2 + x], 14 + i, recv, (z_to * 2 + x_to, rad))
 
     window_copies = [
         panels(block, land.at[(8 - dz) * 2 + x], i, 0, place(dz, dx)) for i, (dz, dx) in enumerate(window)
@@ -298,11 +300,12 @@
 
     @pl.when(gap)
     def _():
-        for recv, low, high in far_regions:
-
-            @pl.when(direct & (slot_k >= low) & (slot_k < high))
-            def _():
-                direct_copy(recv).start()
+        for i, k in enumerate(slots):
+            for recv, low, high in far_regions:
+
+                @pl.when((k >= low) & (k < high))
+                def _():
+                    direct_copy(i, recv).start()
 
         for copy in window_copies:
             copy.start()
@@ -376,8 +379,8 @@
 
     two_up = panels(land.at[pl.ds(12, 6)], land.at[pl.ds(6, 6)], 10, 1, place(3, 0))
     two_down = panels(land.at[pl.ds(16, 6)], land.at[pl.ds(22, 6)], 11, 2, place(-3, 0))
-    three_up = panels(land.at[pl.ds(6, 6)], land.at[pl.ds(0, 6)], 12, 3, place(3, 0))
-    three_down = panels(land.at[pl.ds(22, 4)], land.at[pl.ds(28, 4)], 13, 4, place(-3, 0))
+    part_up = panels(part_out.at[0], part_in.at[0], 12, 3, place(3, 0))
+    part_down = panels(part_out.at[1], part_in.at[1], 13, 4, place(-3, 0))
 
     def when_start(flag, copy):
         @pl.when(flag)
@@ -400,26 +403,13 @@
     reluct_outer()
     first_outer()
 
-    @pl.when(gap)
-    def _():
-        region(6, 12, 1).wait()
-        region(22, 28, 2).wait()
-        when_start(up_ok, three_up)
-        when_start(down_ok, three_down)
-
-    @pl.when(late)
-    def _():
-        second_inner()
-
-    second_outer()
-
-    def deposit(low, high):
+    def deposit(low, high, tile):
         @pl.loop(low // 2, high // 2)
         def _(pair):
             hits, values = [], []
             for slot in (2 * pair, 2 * pair + 1):
                 for part in (0, 1):
-                    cell = land[slot, 18 + part : 19 + part, :].astype(jnp.int32) - az * rows
+                    cell = land[slot, 18 + part : 19 + part, :].astype(jnp.int32) - tile * rows
                     cell = jnp.where(cell < 0, cell + cells, cell)
                     ahead = jnp.where(cell < rows + 8, cell, -1)
                     cell = jnp.where(cell >= cells - 8, cell - (cells - 8) + rows + 8, ahead)
@@ -434,14 +424,37 @@
             second = rest.astype(jnp.bfloat16)
             third = (rest - second.astype(F32)).astype(jnp.bfloat16)
             acc[...] += lax.dot_general(
-                jnp.concatenate(hits, axis=1), jnp.concatenate([first, second, third], axis=0),
+                jnp.concatenate([first, second, third], axis=0), jnp.concatenate(hits, axis=1),
                 (((1,), (1,)), ((), ())), preferred_element_type=F32)
 
+    def deposited():
+        return acc[0:NF, :] + acc[16 : 16 + NF, :] + acc[32 : 32 + NF, :]
+
+    def pass_on(flag, i, low, high, dz, copy):
+        @pl.when(flag)
+        def _():
+            acc[...] = jnp.zeros_like(acc)
+            deposit(low, high, (z + dz + n_z) % n_z * 2 + x)
+            part_out[i] = deposited()
+            copy.start()
+
     @pl.when(gap)
     def _():
+        region(6, 12, 1).wait()
+        pass_on(up_ok, 0, 6, 12, 3, part_up)
+        region(22, 28, 2).wait()
+        pass_on(down_ok, 1, 22, 26, -3, part_down)
+
+    @pl.when(late)
+    def _():
+        second_inner()
+
+    second_outer()
+
+    @pl.when(gap)
+    def _():
         acc[...] = jnp.zeros_like(acc)
-        spread[...] = jnp.zeros_like(spread)
-        deposit(6, 28)
+        deposit(6, 28, az)
 
     @pl.when(has_right)
     def _():
@@ -515,16 +528,23 @@
 
     @pl.when(gap)
     def _():
-        region(0, 6, 3).wait()
-        region(28, 32, 4).wait()
-        deposit(0, 6)
-        deposit(28, 32)
-        spread[0 : rows + 8, 0:48] = acc[0 : rows + 8, :]
-        spread[STRIP - 8 : STRIP, 0:48] = acc[rows + 8 : rows + 16, :]
-        turned = jnp.concatenate(
-            [spread[i * LANES : (i + 1) * LANES, :].T for i in range(3)], axis=1
-        )
-        airgap = turned[0:16] + turned[16:32] + turned[32:48]
+        @pl.when(z < SERVED)
+        def _():
+            region(0, 6, 3).wait()
+            region(28, 32, 4).wait()
+            deposit(0, 6, az)
+            deposit(28, 32, az)
+            spread[0:NF, 0 : rows + 16] = deposited()
+
+        @pl.when(z >= SERVED)
+        def _():
+            part_up.wait_recv()
+            part_down.wait_recv()
+            spread[0:NF, 0 : rows + 16] = deposited() + (part_in[0] + part_in[1])
+
+        summed = spread[...]
+        lanes_of = lax.broadcasted_iota(jnp.int32, (16, STRIP), 1)
+        airgap = jnp.where(lanes_of >= STRIP - 8, pltpu.roll(summed, STRIP - rows - 16, 1), summed)
 
         @pl.when(rad == stator)
         def _():
@@ -567,19 +587,21 @@
         for copy in window_copies:
             copy.wait_send()
 
-        @pl.when(direct)
-        def _():
-            direct_copy(1).wait_send()
+        for i in range(len(served)):
+
+            @pl.when(direct[i])
+            def _():
+                direct_copy(i, 1).wait_send()
 
         @pl.when(up_ok)
         def _():
             two_up.wait_send()
-            three_up.wait_send()
+            part_up.wait_send()
 
         @pl.when(down_ok)
         def _():
             two_down.wait_send()
-            three_down.wait_send()
+            part_down.wait_send()
 
 
 def local(potential, current, material, nu_table, sat_table, panel_flux, panel_jitter, rotor_offset):
@@ -603,10 +625,11 @@
             vmem(TO_LEFT, rows), vmem(TO_LEFT, LANES), vmem(TO_RIGHT, rows), vmem(TO_RIGHT, LANES),
             vmem(NF, 16, STRIP), vmem(L, 16, STRIP), vmem(NF, 16, STRIP),
             vmem(L, 16, STRIP), vmem(L, 16, STRIP), vmem(NF, 16, STRIP),
-            vmem(24, LANES), vmem(32, 24, LANES), vmem(rows + 16, 48), vmem(STRIP, LANES), vmem(LANES, rows),
+            vmem(20, LANES), vmem(32, 20, LANES), vmem(48, rows + 16), vmem(16, STRIP), vmem(LANES, rows),
+            vmem(2, NF, rows + 16), vmem(2, NF, rows + 16),
             pltpu.SemaphoreType.DMA((7,)), pltpu.SemaphoreType.DMA((2,)), pltpu.SemaphoreType.DMA((2,)),
             pltpu.SemaphoreType.DMA((4,)), pltpu.SemaphoreType.DMA((4,)),
-            pltpu.SemaphoreType.DMA((14,)), pltpu.SemaphoreType.DMA((5,)),
+            pltpu.SemaphoreType.DMA((14 + 2 * SERVED,)), pltpu.SemaphoreType.DMA((5,)),
         ],
         compiler_params=pltpu.CompilerParams(
             collective_id=0, has_side_effects=True, vmem_limit_bytes=48 * 1024 * 1024

time: 33.2 us -> 30 us (0.904)
  the two profiles are of different devices: /device:TPU:18 before, /device:TPU:48 now
where the time goes in v3:
time: 30 us; the launch traced here: 29.8 us
  Pallas kernels  28.1 us (94%)
  local copies, waits for them, and re-layouts  1.02 us (3%)
  between operations  0.66 us (2%)
    pallas_call x1, Pallas kernels, local(): pl.pallas_call(kernel, out_shape=jax.ShapeDtypeStruct((NF, rows, lanes),...  28.1 us
    unnamed x1, local copies, waits for them, and re-layouts  1.02 us

profile of v3, /device:TPU:48, one launch (start us, length us, event | category | flops | bytes accessed | tf_op | source)
XLA Modules:
  0.0 29.8 jit_solution(2025206664048867737)
XLA Ops:
  0.7 28.1 %shard_map.82 = f32[9,256,128]{2,1,0:T(8,128)S(1)} custom-call(f32[9,256,128]{2,1,0:T(8,128)} %bitcast.4, f32[9,256,128]{2,1,0:T(8,128)} %bitcast.5, s32[3,256,128]{2,1,0:T(8,128)} %mat.1, f32[8]{0:T(128)} %nu_hbm.1, f32[8]{0:T(128)} %sat_hbm.1, f32[9,256]{1,0:T(8,128)} %flux_hbm.1, s32[256]{0:T(256)} %jitter_hbm.1, s32[1]{0:T(128)S(6)} %copy.10.offset), custom_call_target="tpu_custom_call" | custom-call | tf_op jit(solution)/shard_map/pallas_call | solution.py:613
  28.8 1.0 %copy.11 = f32[3,3,256,128]{3,2,1,0:T(8,128)} copy(f32[3,3,256,128]{3,2,1,0:T(8,128)S(1)} %bitcast.3) | data formatting | bytes 2359296

commit v4 on v3

--- a/solution.py
+++ b/solution.py
@@ -400,9 +400,6 @@
         reluct_inner()
         first_inner()
 
-    reluct_outer()
-    first_outer()
-
     def deposit(low, high, tile):
         @pl.loop(low // 2, high // 2)
         def _(pair):
@@ -444,6 +441,9 @@
         pass_on(up_ok, 0, 6, 12, 3, part_up)
         region(22, 28, 2).wait()
         pass_on(down_ok, 1, 22, 26, -3, part_down)
+
+    reluct_outer()
+    first_outer()
 
     @pl.when(late)
     def _():

time: 30 us -> 31.2 us (1.040)
  Pallas kernels: 28.1 us -> 29.3 us
    pallas_call x1, Pallas kernels: 28.1 us -> 29.3 us  [local(): pl.pallas_call(kernel, out_shape=jax.ShapeDtypeStruct((NF, rows, lanes),...]
where the time goes in v4:
time: 31.2 us; the launch traced here: 31 us
  Pallas kernels  29.3 us (94%)
  local copies, waits for them, and re-layouts  1.02 us (3%)
  between operations  0.66 us (2%)
    pallas_call x1, Pallas kernels, local(): pl.pallas_call(kernel, out_shape=jax.ShapeDtypeStruct((NF, rows, lanes),...  29.3 us
    unnamed x1, local copies, waits for them, and re-layouts  1.02 us

profile of v4, /device:TPU:48, one launch (start us, length us, event | category | flops | bytes accessed | tf_op | source)
XLA Modules:
  0.0 31.0 jit_solution(16909127451611984463)
XLA Ops:
  0.7 29.3 %shard_map.82 = f32[9,256,128]{2,1,0:T(8,128)S(1)} custom-call(f32[9,256,128]{2,1,0:T(8,128)} %bitcast.4, f32[9,256,128]{2,1,0:T(8,128)} %bitcast.5, s32[3,256,128]{2,1,0:T(8,128)} %mat.1, f32[8]{0:T(128)} %nu_hbm.1, f32[8]{0:T(128)} %sat_hbm.1, f32[9,256]{1,0:T(8,128)} %flux_hbm.1, s32[256]{0:T(256)} %jitter_hbm.1, s32[1]{0:T(128)S(6)} %copy.10.offset), custom_call_target="tpu_custom_call" | custom-call | tf_op jit(solution)/shard_map/pallas_call | solution.py:613
  30.0 1.0 %copy.11 = f32[3,3,256,128]{3,2,1,0:T(8,128)} copy(f32[3,3,256,128]{3,2,1,0:T(8,128)S(1)} %bitcast.3) | data formatting | bytes 2359296
